TPU v7x, 32 devices: a whole 2x2x4 slice. The times are simulated.
32 devices in a mesh: slab: 16 (over z, x, core), tp: 2 (over y).
Axes of the slice: x: 2, y: 2, z: 4, core: 2. Of those that a mesh axis runs over, the one named last changes fastest.
Arguments:
- tokens: bfloat16 [16384, 512], P('slab', 'tp'), may hold values from -8 to 8
- stem_taps: float32 [3, 512], P(None, 'tp'), may hold values from 0.1 to 1.9
- query_weight: bfloat16 [512, 512], P(None, 'tp'), may hold values from -0.25 to 0.25
- key_weight: bfloat16 [512, 512], P(None, 'tp'), may hold values from -0.25 to 0.25
- value_weight: bfloat16 [512, 512], P(None, 'tp'), may hold values from -0.25 to 0.25
- out_weight: bfloat16 [512, 512], P('tp'), may hold values from -0.25 to 0.25
- key_blocks: int32 [128, 4], P('slab'), may hold values from 0 to 127, as said below
- counts: int32 [128], P('slab'), may hold values from 3 to 4, as said below
- cotangent: bfloat16 [16384, 512], P('slab', 'tp'), may hold values from -6 to 6
Outputs:
- layer_out: bfloat16 [16384, 512], P('slab', 'tp')
- grad_tokens: float32 [16384, 512], P('slab', 'tp')
- grad_taps: float32 [3, 512], P(None, 'tp')
- grad_query_weight: float32 [512, 512], P(None, 'tp')
- grad_key_weight: float32 [512, 512], P(None, 'tp')
- grad_value_weight: float32 [512, 512], P(None, 'tp')
- grad_out_weight: float32 [512, 512], P('tp')
Inputs may be any that keep to these rules, and one draw needn't show every extreme that they name: `key_blocks`: query block i lies in plane p = i // 4. Its slots 0, 1, 2 name the block at the same position in planes p, p - 1 and p + 1 (planes modulo 32); every live slot names a different block of these three planes; slots from counts[i] on name block i itself. `counts`: some query block has all 4 slots live; loads differ from plane to plane.
All inputs are finite; a program needn't handle non-finite values.
Results may differ from a plain program's by a relative error of at most 0.009.
The roundings to bfloat16 on the way count: a program that leaves them out, or rounds other values in their place, can miss the bound.
Values may be sent and summed in bfloat16 or wider, within the bound.
A program may use at most 128 MiB of HBM per device.

v0:
```python
import jax
import jax.numpy as jnp
from jax import lax
from jax.sharding import PartitionSpec as P

HD = 64
BLK = 128
PLANE_TOK = 512
MAXK = 4


NEG = -1e30


def extended(block, sides, width):
    for axis, dim in sides:
        count = lax.axis_size(axis)
        forward = [(i, i + 1) for i in range(count - 1)]
        forward.append((count - 1, 0))
        backward = [(target, source) for source, target in forward]
        low = lax.ppermute(
            lax.slice_in_dim(block, block.shape[dim] - width, None, axis=dim), axis, forward
        )
        high = lax.ppermute(lax.slice_in_dim(block, 0, width, axis=dim), axis, backward)
        block = jnp.concatenate([low, block, high], axis=dim)
    return block


def shifted(shard, axis, by):
    size = lax.axis_size(axis)
    return lax.ppermute(shard, axis, [(i, (i + by) % size) for i in range(size)])


def softmax_scores(query_block, key_block, live_counts, score_scale):
    scores = (
        jnp.einsum("gqhd,gkhd->ghqk", query_block, key_block, preferred_element_type=jnp.float32)
        * score_scale
    )
    slot_ids = jnp.arange(key_block.shape[1]) // BLK
    live_mask = slot_ids[None, :] < live_counts[:, None]
    scores = jnp.where(live_mask[:, None, None, :], scores, NEG)
    row_max = jnp.max(scores, axis=-1, keepdims=True)
    exp_scores = jnp.exp(scores - row_max)
    return exp_scores / jnp.sum(exp_scores, axis=-1, keepdims=True)


def body(
    tokens,
    stem_taps,
    query_weight,
    key_weight,
    value_weight,
    out_weight,
    key_blocks,
    counts,
    cotangent,
):
    token_count = tokens.shape[0]
    plane_rows = PLANE_TOK
    slab_count = lax.axis_size("slab")
    local_planes = token_count // plane_rows
    plane_total = local_planes * slab_count
    per_plane = plane_rows // BLK
    head_cols = query_weight.shape[1]
    heads_local = head_cols // HD
    score_scale = HD ** (-0.5)
    narrow = extended(tokens, (("slab", 0),), plane_rows)
    inputs_f = narrow.astype(jnp.float32)
    stem_own = (
        stem_taps[0] * inputs_f[:token_count]
        + stem_taps[1] * inputs_f[plane_rows : plane_rows + token_count]
        + stem_taps[2] * inputs_f[2 * plane_rows :]
    ).astype(jnp.bfloat16)
    stem_full, grad_rows = (
        lax.all_gather(stem_own, "tp", axis=1, tiled=True),
        lax.all_gather(cotangent, "tp", axis=1, tiled=True),
    )
    query_rows = jnp.dot(stem_full, query_weight, preferred_element_type=jnp.float32).astype(
        jnp.bfloat16
    )
    key_rows = jnp.dot(stem_full, key_weight, preferred_element_type=jnp.float32).astype(
        jnp.bfloat16
    )
    value_rows = jnp.dot(stem_full, value_weight, preferred_element_type=jnp.float32).astype(
        jnp.bfloat16
    )
    packed = jnp.stack([key_rows, value_rows])
    packed_ext = extended(packed, (("slab", 1),), plane_rows)
    keys_ext = packed_ext[0]
    values_ext = packed_ext[1]
    first_plane = lax.axis_index("slab") * local_planes
    block_plane = key_blocks // per_plane
    rel_plane = jnp.remainder(block_plane - first_plane + 1, plane_total)
    local_blocks = rel_plane * per_plane + jnp.remainder(key_blocks, per_plane)
    key_table = keys_ext.reshape(-1, BLK, heads_local, HD)
    value_table = values_ext.reshape(-1, BLK, heads_local, HD)
    ext_count = key_table.shape[0]
    groups = token_count // BLK // 4
    query_groups = query_rows.reshape(groups, 4, BLK, heads_local, HD)
    index_groups = local_blocks.reshape(groups, 4, MAXK)
    count_groups = counts.reshape(groups, 4)

    def fetch(table, block_ids):
        picked = jnp.take(table, block_ids.reshape(-1), axis=0)
        return picked.reshape(4, MAXK * BLK, heads_local, HD)

    def forward_group(inputs):
        query_block, block_ids, live_counts = inputs
        key_block = fetch(key_table, block_ids)
        value_block = fetch(value_table, block_ids)
        attn_probs = softmax_scores(query_block, key_block, live_counts, score_scale)
        probs_low = attn_probs.astype(jnp.bfloat16)
        return jnp.einsum(
            "ghqk,gkhd->gqhd", probs_low, value_block, preferred_element_type=jnp.float32
        ).astype(jnp.bfloat16)

    attn = lax.map(forward_group, (query_groups, index_groups, count_groups)).reshape(
        token_count, head_cols
    )
    partial_value = jnp.dot(attn, out_weight, preferred_element_type=jnp.float32)
    mixed_rows = lax.psum_scatter(partial_value, "tp", scatter_dimension=1, tiled=True)
    layer_out = (stem_own.astype(jnp.float32) + mixed_rows).astype(jnp.bfloat16)
    grad_attn = lax.dot_general(
        grad_rows, out_weight, (((1,), (1,)), ((), ())), preferred_element_type=jnp.float32
    ).astype(jnp.bfloat16)
    grad_out_weight = lax.dot_general(
        attn, grad_rows, (((0,), (0,)), ((), ())), preferred_element_type=jnp.float32
    )
    grad_groups = grad_attn.reshape(groups, 4, BLK, heads_local, HD)

    def backward_group(grad_pairs, inputs):
        query_block, block_ids, live_counts, grad_block = inputs
        key_block = fetch(key_table, block_ids)
        value_block = fetch(value_table, block_ids)
        attn_probs = softmax_scores(query_block, key_block, live_counts, score_scale)
        probs_low = attn_probs.astype(jnp.bfloat16)
        grad_probs = jnp.einsum(
            "gqhd,gkhd->ghqk", grad_block, value_block, preferred_element_type=jnp.float32
        )
        row_inner = jnp.sum(attn_probs * grad_probs, axis=-1, keepdims=True)
        grad_scores = (attn_probs * (grad_probs - row_inner) * score_scale).astype(jnp.bfloat16)
        grad_query = jnp.einsum(
            "ghqk,gkhd->gqhd", grad_scores, key_block, preferred_element_type=jnp.float32
        ).astype(jnp.bfloat16)
        grad_key = jnp.einsum(
            "ghqk,gqhd->gkhd", grad_scores, query_block, preferred_element_type=jnp.float32
        )
        grad_value = jnp.einsum(
            "ghqk,gqhd->gkhd", probs_low, grad_block, preferred_element_type=jnp.float32
        )
        slot_rows = jnp.stack([grad_key, grad_value]).reshape(2, 4 * MAXK, BLK, head_cols)
        grad_pairs = grad_pairs.at[:, block_ids.reshape(-1)].add(slot_rows)
        return (grad_pairs, grad_query)

    start_pairs = jnp.zeros((2, ext_count, BLK, head_cols), jnp.float32)
    grad_pairs, grad_query = lax.scan(
        backward_group, start_pairs, (query_groups, index_groups, count_groups, grad_groups)
    )
    grad_query = grad_query.reshape(token_count, head_cols)
    grad_pairs = grad_pairs.reshape(2, ext_count * BLK, head_cols)
    from_next = shifted(grad_pairs[:, :plane_rows], "slab", -1)
    from_prev = shifted(
        grad_pairs[:, plane_rows + token_count :].astype(jnp.bfloat16), "slab", 1
    ).astype(jnp.float32)
    own_rows = grad_pairs[:, plane_rows : plane_rows + token_count]
    own_rows = own_rows.at[:, token_count - plane_rows :].add(from_next)
    own_rows = own_rows.at[:, :plane_rows].add(from_prev)
    grad_key_rows = own_rows[0].astype(jnp.bfloat16)
    grad_value_rows = own_rows[1].astype(jnp.bfloat16)
    contract = (((1,), (1,)), ((), ()))
    partial_input = (
        lax.dot_general(grad_query, query_weight, contract, preferred_element_type=jnp.float32)
        + lax.dot_general(grad_key_rows, key_weight, contract, preferred_element_type=jnp.float32)
        + lax.dot_general(
            grad_value_rows, value_weight, contract, preferred_element_type=jnp.float32
        )
    )
    input_part = lax.psum_scatter(partial_input, "tp", scatter_dimension=1, tiled=True)
    grad_stem = cotangent.astype(jnp.float32) + input_part
    grad_ext = extended(grad_stem.astype(jnp.bfloat16), (("slab", 0),), plane_rows).astype(
        grad_stem.dtype
    )
    grad_tokens = (
        stem_taps[0] * grad_ext[2 * plane_rows :]
        + stem_taps[1] * grad_stem
        + stem_taps[2] * grad_ext[:token_count]
    )
    tap_grads = jnp.stack(
        [
            jnp.sum(grad_stem * inputs_f[:token_count], axis=0),
            jnp.sum(grad_stem * inputs_f[plane_rows : plane_rows + token_count], axis=0),
            jnp.sum(grad_stem * inputs_f[2 * plane_rows :], axis=0),
        ]
    )
    rows_contract = (((0,), (0,)), ((), ()))
    grad_query_weight = lax.dot_general(
        stem_full, grad_query, rows_contract, preferred_element_type=jnp.float32
    )
    grad_key_weight = lax.dot_general(
        stem_full, grad_key_rows, rows_contract, preferred_element_type=jnp.float32
    )
    grad_value_weight = lax.dot_general(
        stem_full, grad_value_rows, rows_contract, preferred_element_type=jnp.float32
    )
    reduced = lax.psum(
        (grad_query_weight, grad_key_weight, grad_value_weight, grad_out_weight, tap_grads), "slab"
    )
    return (layer_out, grad_tokens, reduced[4], reduced[0], reduced[1], reduced[2], reduced[3])


def solution(mesh):
    in_specs = (
        P("slab", "tp"),
        P(None, "tp"),
        P(None, "tp"),
        P(None, "tp"),
        P(None, "tp"),
        P("tp", None),
        P("slab", None),
        P("slab"),
        P("slab", "tp"),
    )
    out_specs = (
        P("slab", "tp"),
        P("slab", "tp"),
        P(None, "tp"),
        P(None, "tp"),
        P(None, "tp"),
        P(None, "tp"),
        P("tp", None),
    )
    return jax.shard_map(body, mesh=mesh, in_specs=in_specs, out_specs=out_specs, check_vma=False)
```

profile of v0, /device:TPU:0, one launch (start us, length us, event | category | flops | bytes accessed | tf_op | source)
XLA Modules:
  0.0 511.7 jit_solution(13610009200440612394)
XLA Ops:
  8.9 5.0 collective-permute-start.1
  22.6 22.0 %all-gather.3.cloned.1.call-done = bf16[1024,512]{1,0:T(8,128)(2,1)} async-done(((bf16[1024,256]{1,0:T(8,128)(2,1)}), bf16[1024,512]{1,0:T(8,128)(2,1)}) %all-gather.3.cloned.1.call-update) | async-done | bytes 1048592 | tf_op jit(solution)/shard_map/all_gather | solution.py:75
  49.0 4.4 collective-permute-start.3
  53.4 13.9 %all-gather.5.cloned.1.call-done = bf16[1024,512]{1,0:T(8,128)(2,1)} async-done(((bf16[1024,256]{1,0:T(8,128)(2,1)}), bf16[1024,512]{1,0:T(8,128)(2,1)}) %all-gather.5.cloned.1.call-update) | async-done | bytes 1048592 | tf_op jit(solution)/shard_map/all_gather | solution.py:76
  86.1 208.6 %while.29 = (s32[]{:T(128)}, f32[2,16,128,256]{3,2,1,0:T(8,128)}, bf16[2,4,128,4,64]{2,1,0,4,3:T(4,128)(2,1)}, s32[2,4,4]{2,1,0:T(4,128)S(1)}, bf16[2,4,128,4,64...) while((s32[]{:T(128)}, f32[2,16,128,256]{3,2,1,0:T(8,128)}, ...), condition=%wide.region_10.12_spmd, body=%wide.region_5.11_spmd.sunk | while | flops 695349952 | bytes 111990032 | solution.py:156
  90.3 5.2 %gather_fusion.2 = bf16[16,128,4,64]{3,2,1,0:T(4,128)(2,1)} fusion(bf16[16,128,4,64]{3,2,1,0:T(4,128)(2,1)} %get-tuple-element.513, s32[1024]{0:T(1024)S(1)} %pad_clamp_fusion.5), kind=kCustom, calls=%fused_computation.3.clone.clone.1 | custom fusion | bytes 2097216 | tf_op jit(solution)/shard_map/while/body/eval_jaxpr/jit(_take)/gather | solution.py:104
  95.5 6.1 %broadcast_select_fusion.7 = (bf16[16,128,4,64]{3,2,1,0:T(4,128)(2,1)}, bf16[16,128,4,64]{3,2,1,0:T(4,128)(2,1)}) fusion(bf16[16,128,4,64]{3,2,1,0:T(4,128)(2,1)} %gather_fusion.2, pred[16]{0:T(512)(128)(4,1)S(1)} %compare_and_fusion.5, bf16[16,128,4,64]{3,2,1,0:T(4,128)(2,1)} %gather_fusion.3), kind=kLoop, calls=%fused_computation.61.clone.1 | loop fusion | flops 1048576 | bytes 4194320 | tf_op jit(solution)/shard_map/while/body/eval_jaxpr/jit(_take)/select_n | solution.py:104
  104.6 4.4 fusion.193
  109.0 4.4 fusion.191
  113.4 17.9 %fusion.195 = bf16[1,4,128,4,64]{2,4,3,1,0:T(8,128)(2,1)} fusion(bf16[4,512,4,64]{1,3,2,0:T(8,128)(2,1)S(1)} %copy.108, f32[4,4,128,512]{3,2,1,0:T(8,128)} %fusion.193, f32[4,4,128,512]{3,2,1,0:T(8,128)} %get-tuple-element.458, f32[4,4,128]{2,1,0:T(4,128)S(1)} %get-tuple-element.459), kind=kOutput, calls=%fused_computation.67.clone.1 | convolution fusion | flops 141691392 | bytes 9707520 | tf_op jit(solution)/shard_map/while/body/eval_jaxpr/ghqk,gkhd->gqhd/dot_general | solution.py:142
  131.4 18.9 %fusion.194 = f32[4,512,4,64]{1,3,2,0:T(8,128)} fusion(f32[4,4,128,512]{3,2,1,0:T(8,128)} %fusion.193, bf16[2,4,128,4,64]{2,4,3,1,0:T(8,128)(2,1)} %get-tuple-element.509, s32[]{:T(128)S(6)} %copy.124, f32[4,4,128,512]{3,2,1,0:T(8,128)} %get-tuple-element.458, f32[4,4,128]{2,1,0:T(4,128)S(1)} %get-tuple-element.459), kind=kOutput, calls=%fused_computation.64.clone.1 | convolution fusion | flops 141560320 | bytes 19152900 | tf_op jit(solution)/shard_map/while/body/eval_jaxpr/ghqk,gqhd->gkhd/dot_general | solution.py:145
  166.3 4.5 maximum_bitcast_fusion.2
  170.7 5.3 %copy.111 = f32[16,2,128,256]{3,2,1,0:T(8,128)} copy(f32[16,2,128,256]{2,0,3,1:T(8,128)} %maximum_bitcast_fusion.2) | data formatting | bytes 8388608 | tf_op jit(solution)/shard_map/while/body/eval_jaxpr/stack | solution.py:151
  176.0 9.3 %scatter_fusion = f32[2,16,128,256]{3,2,1,0:T(8,128)} fusion(f32[2,16,128,256]{3,2,1,0:T(8,128)} %get-tuple-element.496, s32[16]{0:T(128)S(1)} %fusion.189, f32[16,2,128,256]{3,2,1,0:T(8,128)} %copy.111), kind=kCustom, calls=%fused_computation.4.clone.1 | custom fusion | flops 1048576 | bytes 12582976 | tf_op jit(solution)/shard_map/while/body/eval_jaxpr/scatter-add | solution.py:152
  190.3 5.2 %gather_fusion.2 = bf16[16,128,4,64]{3,2,1,0:T(4,128)(2,1)} fusion(bf16[16,128,4,64]{3,2,1,0:T(4,128)(2,1)} %get-tuple-element.513, s32[1024]{0:T(1024)S(1)} %pad_clamp_fusion.5), kind=kCustom, calls=%fused_computation.3.clone.clone.1 | custom fusion | bytes 2097216 | tf_op jit(solution)/shard_map/while/body/eval_jaxpr/jit(_take)/gather | solution.py:104
  195.6 6.1 %broadcast_select_fusion.7 = (bf16[16,128,4,64]{3,2,1,0:T(4,128)(2,1)}, bf16[16,128,4,64]{3,2,1,0:T(4,128)(2,1)}) fusion(bf16[16,128,4,64]{3,2,1,0:T(4,128)(2,1)} %gather_fusion.2, pred[16]{0:T(512)(128)(4,1)S(1)} %compare_and_fusion.5, bf16[16,128,4,64]{3,2,1,0:T(4,128)(2,1)} %gather_fusion.3), kind=kLoop, calls=%fused_computation.61.clone.1 | loop fusion | flops 1048576 | bytes 4194320 | tf_op jit(solution)/shard_map/while/body/eval_jaxpr/jit(_take)/select_n | solution.py:104
  204.6 4.4 fusion.193
  209.1 4.4 fusion.191
  213.5 17.9 %fusion.195 = bf16[1,4,128,4,64]{2,4,3,1,0:T(8,128)(2,1)} fusion(bf16[4,512,4,64]{1,3,2,0:T(8,128)(2,1)S(1)} %copy.108, f32[4,4,128,512]{3,2,1,0:T(8,128)} %fusion.193, f32[4,4,128,512]{3,2,1,0:T(8,128)} %get-tuple-element.458, f32[4,4,128]{2,1,0:T(4,128)S(1)} %get-tuple-element.459), kind=kOutput, calls=%fused_computation.67.clone.1 | convolution fusion | flops 141691392 | bytes 9707520 | tf_op jit(solution)/shard_map/while/body/eval_jaxpr/ghqk,gkhd->gqhd/dot_general | solution.py:142
  231.4 18.9 %fusion.194 = f32[4,512,4,64]{1,3,2,0:T(8,128)} fusion(f32[4,4,128,512]{3,2,1,0:T(8,128)} %fusion.193, bf16[2,4,128,4,64]{2,4,3,1,0:T(8,128)(2,1)} %get-tuple-element.509, s32[]{:T(128)S(6)} %copy.124, f32[4,4,128,512]{3,2,1,0:T(8,128)} %get-tuple-element.458, f32[4,4,128]{2,1,0:T(4,128)S(1)} %get-tuple-element.459), kind=kOutput, calls=%fused_computation.64.clone.1 | convolution fusion | flops 141560320 | bytes 19152900 | tf_op jit(solution)/shard_map/while/body/eval_jaxpr/ghqk,gqhd->gkhd/dot_general | solution.py:145
  258.9 4.3 copy.110
  266.3 4.5 maximum_bitcast_fusion.2
  270.7 5.3 %copy.111 = f32[16,2,128,256]{3,2,1,0:T(8,128)} copy(f32[16,2,128,256]{2,0,3,1:T(8,128)} %maximum_bitcast_fusion.2) | data formatting | bytes 8388608 | tf_op jit(solution)/shard_map/while/body/eval_jaxpr/stack | solution.py:151
  276.1 9.4 %scatter_fusion = f32[2,16,128,256]{3,2,1,0:T(8,128)} fusion(f32[2,16,128,256]{3,2,1,0:T(8,128)} %get-tuple-element.496, s32[16]{0:T(128)S(1)} %fusion.189, f32[16,2,128,256]{3,2,1,0:T(8,128)} %copy.111), kind=kCustom, calls=%fused_computation.4.clone.1 | custom fusion | flops 1048576 | bytes 12582976 | tf_op jit(solution)/shard_map/while/body/eval_jaxpr/scatter-add | solution.py:152
  306.8 6.5 %collective-permute-done.4 = f32[2,512,256]{2,1,0:T(8,128)} collective-permute-done((f32[2,512,256]{2,1,0:T(8,128)}, f32[2,512,256]{2,1,0:T(8,128)}, u32[]{:S(2)}, u32[]{:S(2)}) %collective-permute-start.4) | collective-permute-done | bytes 1048608 | tf_op jit(solution)/shard_map/ppermute | solution.py:31
  322.9 35.8 %while.28 = (s32[]{:T(128)}, bf16[2,4,128,4,64]{2,1,0,4,3:T(4,128)(2,1)}, s32[2,4,4]{2,1,0:T(4,128)S(1)}, bf16[16,128,4,64]{3,2,1,0:T(4,128)(2,1)}, s32[2,4]{1,0...) while((s32[]{:T(128)}, ...), condition=%wide.region_3.5_spmd, body=%wide.region_0.4_spmd.sunk | while | flops 278011520 | bytes 33583988 | solution.py:117
  326.7 5.1 %gather_fusion = bf16[16,128,4,64]{3,2,1,0:T(4,128)(2,1)} fusion(bf16[16,128,4,64]{3,2,1,0:T(4,128)(2,1)} %get-tuple-element.480, s32[1024]{0:T(1024)S(1)} %pad_clamp_fusion.4), kind=kCustom, calls=%fused_computation.clone.clone.1 | custom fusion | bytes 2097216 | tf_op jit(solution)/shard_map/while/body/eval_jaxpr/jit(_take)/gather | solution.py:104
  344.6 5.2 %gather_fusion = bf16[16,128,4,64]{3,2,1,0:T(4,128)(2,1)} fusion(bf16[16,128,4,64]{3,2,1,0:T(4,128)(2,1)} %get-tuple-element.480, s32[1024]{0:T(1024)S(1)} %pad_clamp_fusion.4), kind=kCustom, calls=%fused_computation.clone.clone.1 | custom fusion | bytes 2097216 | tf_op jit(solution)/shard_map/while/body/eval_jaxpr/jit(_take)/gather | solution.py:104
  372.2 4.4 collective-permute-start.7
  376.7 20.1 %reduce-scatter.3.cloned.1.call-done = f32[1024,256]{1,0:T(8,128)} async-done(((f32[1024,512]{1,0:T(8,128)}), f32[1024,256]{1,0:T(8,128)}) %reduce-scatter.3.cloned.1.call-update) | async-done | bytes 1048592 | tf_op jit(solution)/shard_map/reduce_scatter | solution.py:121
  402.0 34.2 %psum.35 = f32[3,256]{1,0:T(4,128)} all-reduce(f32[3,256]{1,0:T(4,128)S(1)} %pad_maximum_fusion.2), channel_id=1, replica_groups=mesh['slab'=16,'tp'=2] {'slab'}, use_global_device_ids=true, to_apply=%region_15.17 | all-reduce | flops 768 | bytes 6144 | tf_op jit(solution)/shard_map/psum | solution.py:205
  436.1 63.4 %all-reduce.3.cloned.1.call-done = (f32[512,256]{1,0:T(8,128)}, f32[512,256]{1,0:T(8,128)}, f32[512,256]{1,0:T(8,128)}, f32[256,512]{1,0:T(8,128)}) async-done(((f32[512,256]{1,0:T(8,128)}, f32[512,256]{1,0:T(8,128)}, f32[512,256]{1,0:T(8,128)}, f32[256,512]{1,0:T(8,128)}), (f32[512,256]{1,0:T(8,128)}, f32[512,256]{1,0:T(8,128)}, f32[512,256]{1,0:T(8,128)}, ...) | async-done | bytes 2097168 | tf_op jit(solution)/shard_map/psum | solution.py:205
  (215 shorter events, 147.7 us)
Async XLA Ops:
  7.2 65.9 %copy-start = (bf16[512,256]{1,0:T(8,128)(2,1)S(1)}, bf16[512,256]{1,0:T(8,128)(2,1)}, u32[]{:S(2)}) copy-start(bf16[512,256]{1,0:T(8,128)(2,1)} %param.21) | copy-start | bytes 786436
  7.2 37.4 %all-gather.3.cloned.1.call-start = ((), (), s32[]{:S(2)}) async-start(), calls=%async_computation.2 | async-start | bytes 1572864 | tf_op jit(solution)/shard_map/all_gather | solution.py:75
  8.3 9.7 %collective-permute-start = (bf16[512,256]{1,0:T(8,128)(2,1)S(1)}, bf16[512,256]{1,0:T(8,128)(2,1)S(1)}, u32[]{:S(2)}, u32[]{:S(2)}) collective-permute-start(bf16[512,256]{1,0:T(8,128)(2,1)S(1)} %get-tuple-element.342), channel_id=1, source_target_pairs={{0,2},{2,4},{4,6},{6,8},{8,10},{10,12},{12,14},{14,16},{16,18},{18... | collective-permute-start | bytes 786440 | tf_op jit(solution)/shard_map/ppermute | solution.py:21
  8.9 9.1 %collective-permute-start.1 = (bf16[512,256]{1,0:T(8,128)(2,1)S(1)}, bf16[512,256]{1,0:T(8,128)(2,1)S(1)}, u32[]{:S(2)}, u32[]{:S(2)}) collective-permute-start(bf16[512,256]{1,0:T(8,128)(2,1)S(1)} %get-tuple-element.343), channel_id=1, source_target_pairs={{2,0},{4,2},{6,4},{8,6},{10,8},{12,10},{14,12},{16,14},{18,16},{20... | collective-permute-start | bytes 786440 | tf_op jit(solution)/shard_map/ppermute | solution.py:24
  14.7 4.5 copy-start.28
  14.7 4.5 copy-start.30
  20.5 24.0 %copy-start.19 = (bf16[512,256]{1,0:T(8,128)(2,1)S(1)}, bf16[512,256]{1,0:T(8,128)(2,1)}, u32[]{:S(2)}) copy-start(bf16[512,256]{1,0:T(8,128)(2,1)} %param.23) | copy-start | bytes 786436
  21.5 24.7 %copy-start.21 = (bf16[512,256]{1,0:T(8,128)(2,1)S(1)}, bf16[512,256]{1,0:T(8,128)(2,1)}, u32[]{:S(2)}) copy-start(bf16[512,256]{1,0:T(8,128)(2,1)} %param.22) | copy-start | bytes 786436
  21.6 45.8 %all-gather.5.cloned.1.call-start = ((), (), s32[]{:S(2)}) async-start(), calls=%async_computation.4 | async-start | bytes 1572864 | tf_op jit(solution)/shard_map/all_gather | solution.py:76
  22.3 347.4 %reduce-scatter.5.cloned.1.call-start = ((), (), s32[]{:S(2)}) async-start(), calls=%async_computation.5 | async-start | bytes 3145728 | tf_op jit(solution)/shard_map/reduce_scatter | solution.py:178
  46.2 21.1 %copy-start.23 = (bf16[256,512]{1,0:T(8,128)(2,1)S(1)}, bf16[256,512]{1,0:T(8,128)(2,1)}, u32[]{:S(2)}) copy-start(bf16[256,512]{1,0:T(8,128)(2,1)} %param.24) | copy-start | bytes 786436
  49.0 26.2 %collective-permute-start.2 = (bf16[2,512,256]{2,1,0:T(8,128)(2,1)}, bf16[2,512,256]{2,1,0:T(8,128)(2,1)}, u32[]{:S(2)}, u32[]{:S(2)}) collective-permute-start(bf16[2,512,256]{2,1,0:T(8,128)(2,1)} %get-tuple-element.338), channel_id=1, source_target_pairs={{0,2},{2,4},{4,6},{6,8},{8,10},{10,12},{12,14},{14,16},{16,18},{18... | collective-permute-start | bytes 1572872 | tf_op jit(solution)/shard_map/ppermute | solution.py:21
  49.0 24.1 %copy-start.3 = (bf16[1024,512]{1,0:T(8,128)(2,1)S(1)}, bf16[1024,512]{1,0:T(8,128)(2,1)}, u32[]{:S(2)}) copy-start(bf16[1024,512]{1,0:T(8,128)(2,1)} %all-gather.3.cloned.1.call-done) | copy-start | bytes 3145732
  49.0 26.2 %collective-permute-start.3 = (bf16[2,512,256]{2,1,0:T(8,128)(2,1)}, bf16[2,512,256]{2,1,0:T(8,128)(2,1)}, u32[]{:S(2)}, u32[]{:S(2)}) collective-permute-start(bf16[2,512,256]{2,1,0:T(8,128)(2,1)} %get-tuple-element.339), channel_id=1, source_target_pairs={{2,0},{4,2},{6,4},{8,6},{10,8},{12,10},{14,12},{16,14},{18,16},{20... | collective-permute-start | bytes 1572872 | tf_op jit(solution)/shard_map/ppermute | solution.py:24
  131.4 18.9 %copy-start.8 = (bf16[2,4,128,4,64]{2,4,3,1,0:T(8,128)(2,1)S(1)}, bf16[2,4,128,4,64]{2,4,3,1,0:T(8,128)(2,1)}, u32[]{:S(2)}) copy-start(bf16[2,4,128,4,64]{2,4,3,1,0:T(8,128)(2,1)} %get-tuple-element.512) | copy-start | bytes 1572868 | tf_op jit(solution)/shard_map/while
  176.0 9.3 %copy-start.6 = (bf16[1,4,128,4,64]{2,4,3,1,0:T(8,128)(2,1)S(1)}, bf16[1,4,128,4,64]{2,4,3,1,0:T(8,128)(2,1)}, u32[]{:S(2)}) copy-start(bf16[1,4,128,4,64]{2,4,3,1,0:T(8,128)(2,1)} %fusion.195) | copy-start | bytes 786436 | tf_op jit(solution)/shard_map/while
  176.0 9.3 %copy-start.14 = (bf16[2,4,128,4,64]{2,1,0,4,3:T(4,128)(2,1)S(1)}, bf16[2,4,128,4,64]{2,1,0,4,3:T(4,128)(2,1)}, u32[]{:S(2)}) copy-start(bf16[2,4,128,4,64]{2,1,0,4,3:T(4,128)(2,1)} %get-tuple-element.497) | copy-start | bytes 1572868 | tf_op jit(solution)/shard_map/while
  231.4 18.9 %copy-start.8 = (bf16[2,4,128,4,64]{2,4,3,1,0:T(8,128)(2,1)S(1)}, bf16[2,4,128,4,64]{2,4,3,1,0:T(8,128)(2,1)}, u32[]{:S(2)}) copy-start(bf16[2,4,128,4,64]{2,4,3,1,0:T(8,128)(2,1)} %get-tuple-element.512) | copy-start | bytes 1572868 | tf_op jit(solution)/shard_map/while
  276.1 9.4 %copy-start.6 = (bf16[1,4,128,4,64]{2,4,3,1,0:T(8,128)(2,1)S(1)}, bf16[1,4,128,4,64]{2,4,3,1,0:T(8,128)(2,1)}, u32[]{:S(2)}) copy-start(bf16[1,4,128,4,64]{2,4,3,1,0:T(8,128)(2,1)} %fusion.195) | copy-start | bytes 786436 | tf_op jit(solution)/shard_map/while
  276.1 9.4 %copy-start.14 = (bf16[2,4,128,4,64]{2,1,0,4,3:T(4,128)(2,1)S(1)}, bf16[2,4,128,4,64]{2,1,0,4,3:T(4,128)(2,1)}, u32[]{:S(2)}) copy-start(bf16[2,4,128,4,64]{2,1,0,4,3:T(4,128)(2,1)} %get-tuple-element.497) | copy-start | bytes 1572868 | tf_op jit(solution)/shard_map/while
  297.0 16.2 %collective-permute-start.4 = (f32[2,512,256]{2,1,0:T(8,128)}, f32[2,512,256]{2,1,0:T(8,128)}, u32[]{:S(2)}, u32[]{:S(2)}) collective-permute-start(f32[2,512,256]{2,1,0:T(8,128)} %slice.161), channel_id=1, source_target_pairs={{0,30},{2,0},{4,2},{6,4},{8,6},{10,8},{12,10},{14,12},{16,14},{18,... | collective-permute-start | bytes 3145736 | tf_op jit(solution)/shard_map/ppermute | solution.py:31
  306.2 7.1 %copy-start.5 = (f32[2,1024,256]{2,1,0:T(8,128)S(1)}, f32[2,1024,256]{2,1,0:T(8,128)}, u32[]{:S(2)}) copy-start(f32[2,1024,256]{2,1,0:T(8,128)} %slice.159) | copy-start | bytes 6291460
  306.2 11.6 %collective-permute-start.5 = (bf16[2,512,256]{2,1,0:T(8,128)(2,1)}, bf16[2,512,256]{2,1,0:T(8,128)(2,1)S(1)}, u32[]{:S(2)}, u32[]{:S(2)}) collective-permute-start(bf16[2,512,256]{2,1,0:T(8,128)(2,1)} %slice.203), channel_id=1, source_target_pairs={{0,2},{2,4},{4,6},{6,8},{8,10},{10,12},{12,14},{14,16},{16,18},{18... | collective-permute-start | bytes 1572872 | tf_op jit(solution)/shard_map/ppermute | solution.py:31
  321.9 74.9 %reduce-scatter.3.cloned.1.call-start = ((), (), s32[]{:S(2)}) async-start(), calls=%async_computation.3 | async-start | bytes 3145728 | tf_op jit(solution)/shard_map/reduce_scatter | solution.py:121
  362.9 136.7 %all-reduce.3.cloned.1.call-start = ((), (), s32[]{:S(2)}) async-start(), calls=%async_computation.6 | async-start | bytes 4194304 | tf_op jit(solution)/shard_map/psum | solution.py:205
  369.6 27.2 %copy-start.2 = (f32[2048,256]{1,0:T(8,128)S(1)}, f32[2048,256]{1,0:T(8,128)}, u32[]{:S(2)}) copy-start(f32[2048,256]{1,0:T(8,128)} %copy-done.1) | copy-start | bytes 6291460
  369.6 27.2 %copy-start.27 = (f32[1,256]{1,0:T(1,128)S(1)}, f32[1,256]{1,0:T(1,128)}, u32[]{:S(2)}) copy-start(f32[1,256]{1,0:T(1,128)} %copy-done.26) | copy-start | bytes 3076
  369.6 27.2 %copy-start.29 = (f32[1,256]{1,0:T(1,128)S(1)}, f32[1,256]{1,0:T(1,128)}, u32[]{:S(2)}) copy-start(f32[1,256]{1,0:T(1,128)} %copy-done.28) | copy-start | bytes 3076
  369.6 27.2 %copy-start.31 = (f32[1,256]{1,0:T(1,128)S(1)}, f32[1,256]{1,0:T(1,128)}, u32[]{:S(2)}) copy-start(f32[1,256]{1,0:T(1,128)} %copy-done.30) | copy-start | bytes 3076
  372.2 26.9 %collective-permute-start.6 = (bf16[512,256]{1,0:T(8,128)(2,1)}, bf16[512,256]{1,0:T(8,128)(2,1)}, u32[]{:S(2)}, u32[]{:S(2)}) collective-permute-start(bf16[512,256]{1,0:T(8,128)(2,1)} %get-tuple-element.340), channel_id=1, source_target_pairs={{0,2},{2,4},{4,6},{6,8},{8,10},{10,12},{12,14},{14,16},{16,18},{18... | collective-permute-start | bytes 786440 | tf_op jit(solution)/shard_map/ppermute | solution.py:21
  372.2 26.9 %collective-permute-start.7 = (bf16[512,256]{1,0:T(8,128)(2,1)}, bf16[512,256]{1,0:T(8,128)(2,1)}, u32[]{:S(2)}, u32[]{:S(2)}) collective-permute-start(bf16[512,256]{1,0:T(8,128)(2,1)} %get-tuple-element.341), channel_id=1, source_target_pairs={{2,0},{4,2},{6,4},{8,6},{10,8},{12,10},{14,12},{16,14},{18,16},{20... | collective-permute-start | bytes 786440 | tf_op jit(solution)/shard_map/ppermute | solution.py:24
  499.6 4.6 copy-start.24
  (21 other events, 38.8 us)
Sparse Core Ops, SparseCore 0:
  21.7 22.8 all-gather.2
  46.1 21.2 all-gather.4
  322.0 33.8 reduce-scatter.4
  363.0 33.7 reduce-scatter.2
  401.2 98.3 all-reduce.2
where the time goes:
time: 521 us; the launch traced here: 512 us
  waiting for transfers between devices  133 us (26%)
  local copies, waits for them, and re-layouts  119 us (23%)
  matrix products  119 us (23%)
  other arithmetic  65.1 us (12%)
  blocking collectives  34.2 us (7%)
  starting transfers between devices  18.5 us (4%)
  between operations  14.3 us (3%)
  loops' own time  8.71 us (2%)
    psum x1, waiting for transfers between devices, body(): lax.psum((grad_query_weight, grad_key_weight, grad_value_weight, grad_out...  63.4 us
    dot_general x2, matrix products, backward_group(): jnp.einsum('ghqk,gqhd->gkhd', grad_scores, query_block, preferred_element...  37.9 us
    dot_general x2, matrix products, backward_group(): jnp.einsum('ghqk,gkhd->gqhd', grad_scores, key_block, preferred_element_t...  35.8 us
    gather x8, local copies, waits for them, and re-layouts, fetch(): picked = jnp.take(table, block_ids.reshape(-1), axis=0)  35.1 us
    psum x1, blocking collectives, body(): lax.psum((grad_query_weight, grad_key_weight, grad_value_weight, grad_out...  34.2 us
    another operation x6, local copies, waits for them, and re-layouts, backward_group(): jnp.stack([grad_key, grad_value]).reshape(2, 4 * MAXK, BLK, head_cols)  23.1 us
    all_gather x1, waiting for transfers between devices, body(): lax.all_gather(stem_own, 'tp', axis=1, tiled=True)  22 us
    select_n x8, other arithmetic, fetch(): picked = jnp.take(table, block_ids.reshape(-1), axis=0)  20.6 us
  transfers between devices with their start and end apart: 13, of which 7 were waited for; matrix products, arithmetic and copies ran while one was open for 14% of the time, Pallas kernels for 0%

commit v1 on v0

v1 whole, which is shorter than its diff:
```python
import functools

import jax
import jax.numpy as jnp
from jax import lax
from jax.experimental import pallas as pl
from jax.experimental.pallas import tpu as pltpu
from jax.sharding import PartitionSpec as P

HD = 64
BLK = 128
PLANE_TOK = 512
MAXK = 4
NEG = -1e30
F32 = jnp.float32
BF16 = jnp.bfloat16
MESH = pl.DeviceIdType.MESH
VMEM = pl.BlockSpec(memory_space=pltpu.VMEM)
SMEM = pl.BlockSpec(memory_space=pltpu.SMEM)
ANY = pl.BlockSpec(memory_space=pl.ANY)
LIMIT = 60 * 1024 * 1024
CHUNK = 256


def mm(a, b):
    return jnp.dot(a, b, preferred_element_type=F32)


def mm_nt(a, b):
    return lax.dot_general(a, b, (((1,), (1,)), ((), ())), preferred_element_type=F32)


def mm_tn(a, b):
    return lax.dot_general(a, b, (((0,), (0,)), ((), ())), preferred_element_type=F32)


def part(index, width):
    return pl.ds(pl.multiple_of(index * width, width), width)


def project_kernel(so_ref, st_ref, wq_ref, wk_ref, wv_ref, q_ref, kv_ref):
    tp = lax.axis_index("tp")
    width = so_ref.shape[1]
    cols = wq_ref.shape[1]
    mine, other = part(tp, width), part(1 - tp, width)

    @pl.loop(0, so_ref.shape[0] // CHUNK)
    def _(step):
        rows = part(step, CHUNK)
        so, st = so_ref[rows, :], st_ref[rows, :]

        def project(w_ref):
            return (mm(so, w_ref[mine, :]) + mm(st, w_ref[other, :])).astype(BF16)

        q_ref[rows, :] = project(wq_ref)
        kv_ref[rows, 0:cols] = project(wk_ref)
        kv_ref[rows, cols : 2 * cols] = project(wv_ref)


def attention_kernel(
    slabs,
    blocks_ref,
    counts_ref,
    q_ref,
    kv_ref,
    kv_prev_ref,
    kv_next_ref,
    co_ref,
    ct_ref,
    ow_ref,
    gq_ref,
    gkv_ref,
    gprev_ref,
    gnext_ref,
    mix_ref,
    mix_other_ref,
    gow_ref,
    ext,
    acc,
    grad,
    attn,
    sems,
):
    tp = lax.axis_index("tp")
    slab = lax.axis_index("slab")
    tokens, cols = q_ref.shape
    width = co_ref.shape[1]
    heads = cols // HD
    planes = tokens // PLANE_TOK
    per_plane = PLANE_TOK // BLK
    total = planes * slabs
    copies = [
        pltpu.make_async_copy(kv_prev_ref, ext.at[0:PLANE_TOK], sems.at[0]),
        pltpu.make_async_copy(kv_ref, ext.at[PLANE_TOK : PLANE_TOK + tokens], sems.at[1]),
        pltpu.make_async_copy(
            kv_next_ref, ext.at[PLANE_TOK + tokens : 2 * PLANE_TOK + tokens], sems.at[2]
        ),
    ]
    for copy in copies:
        copy.start()
    mine, other = part(tp, width), part(1 - tp, width)

    @pl.loop(0, tokens // CHUNK)
    def _(step):
        rows = part(step, CHUNK)
        grad[rows, :] = (
            mm_nt(co_ref[rows, :], ow_ref[:, mine]) + mm_nt(ct_ref[rows, :], ow_ref[:, other])
        ).astype(BF16)

    @pl.loop(0, acc.shape[0] // BLK)
    def _(step):
        acc[part(step, BLK), :] = jnp.zeros((BLK, 2 * cols), F32)

    for copy in copies:
        copy.wait()

    lane = lax.broadcasted_iota(jnp.int32, (1, cols), 1) // HD
    masks = [(lane == h).astype(F32).astype(BF16) for h in range(heads)]
    slot = lax.broadcasted_iota(jnp.int32, (1, MAXK * BLK), 1)

    def stack(block):
        return jnp.concatenate([block * mask for mask in masks], axis=0)

    def pick(value):
        out = value[0:BLK]
        for h in range(1, heads):
            out = jnp.where(lane == h, value[h * BLK : (h + 1) * BLK], out)
        return out

    @pl.loop(0, tokens // BLK)
    def _(i):
        rows = part(i, BLK)
        where = []
        for j in range(MAXK):
            block = blocks_ref[i, j]
            plane = lax.rem(
                lax.div(block, per_plane) - slab * planes + 1 + total, total
            )
            where.append(part(plane * per_plane + lax.rem(block, per_plane), BLK))
        keys = jnp.concatenate([ext[at, 0:cols] for at in where], axis=0)
        values = jnp.concatenate([ext[at, cols : 2 * cols] for at in where], axis=0)
        queries = stack(q_ref[rows, :] * jnp.asarray(HD**-0.5, BF16))
        grads = stack(grad[rows, :])
        scores = mm_nt(queries, keys)
        scores = jnp.where(slot < counts_ref[i] * BLK, scores, NEG)
        exps = jnp.exp(scores - jnp.max(scores, axis=-1, keepdims=True))
        probs = exps * (1.0 / jnp.sum(exps, axis=-1, keepdims=True))
        low = probs.astype(BF16)
        attn[rows, :] = pick(mm(low, values)).astype(BF16)
        gprobs = mm_nt(grads, values)
        inner = jnp.sum(probs * gprobs, axis=-1, keepdims=True)
        gscores = (probs * (gprobs - inner)).astype(BF16)
        gq_ref[rows, :] = (pick(mm(gscores, keys)) * (HD**-0.5)).astype(BF16)
        gkeys = mm_tn(gscores, queries)
        gvalues = mm_tn(low, grads)
        for j in range(MAXK):
            acc[where[j], 0:cols] += gkeys[j * BLK : (j + 1) * BLK]
            acc[where[j], cols : 2 * cols] += gvalues[j * BLK : (j + 1) * BLK]

    gprev_ref[...] = acc[0:PLANE_TOK, :].astype(BF16)
    gkv_ref[...] = acc[PLANE_TOK : PLANE_TOK + tokens, :]
    gnext_ref[...] = acc[PLANE_TOK + tokens : 2 * PLANE_TOK + tokens, :].astype(BF16)

    @pl.loop(0, tokens // CHUNK)
    def _(step):
        rows = part(step, CHUNK)
        mix_ref[rows, :] = mm(attn[rows, :], ow_ref[:, mine])
        mix_other_ref[rows, :] = mm(attn[rows, :], ow_ref[:, other]).astype(BF16)

    halves = width // 128
    for index, c_ref in ((tp, co_ref), (1 - tp, ct_ref)):
        product = mm_tn(attn[...], c_ref[...])
        for half in range(halves):
            gow_ref[part(index * halves + half, cols), :] = product[
                :, half * 128 : (half + 1) * 128
            ]


def gradient_kernel(
    gq_ref,
    gkv_ref,
    from_prev_ref,
    from_next_ref,
    so_ref,
    st_ref,
    wq_ref,
    wk_ref,
    wv_ref,
    part_ref,
    part_other_ref,
    gw_ref,
    low,
):
    tp = lax.axis_index("tp")
    tokens, cols = gq_ref.shape
    width = so_ref.shape[1]
    depth = wq_ref.shape[0]
    mine, other = part(tp, width), part(1 - tp, width)
    low[...] = gkv_ref[...].astype(BF16)
    last = tokens - PLANE_TOK
    if last > 0:
        low[0:PLANE_TOK, :] = (gkv_ref[0:PLANE_TOK, :] + from_prev_ref[...].astype(F32)).astype(
            BF16
        )
        low[last:, :] = (gkv_ref[last:, :] + from_next_ref[...].astype(F32)).astype(BF16)
    else:
        low[...] = (
            gkv_ref[...] + from_prev_ref[...].astype(F32) + from_next_ref[...].astype(F32)
        ).astype(BF16)

    @pl.loop(0, tokens // CHUNK)
    def _(step):
        rows = part(step, CHUNK)
        gq = gq_ref[rows, :]
        gk = low[rows, 0:cols]
        gv = low[rows, cols : 2 * cols]

        def back(at):
            return (
                mm_nt(gq, wq_ref[at, :]) + mm_nt(gk, wk_ref[at, :]) + mm_nt(gv, wv_ref[at, :])
            )

        part_ref[rows, :] = back(mine)
        part_other_ref[rows, :] = back(other).astype(BF16)

    halves = cols // 128
    for index, s_ref in ((tp, so_ref), (1 - tp, st_ref)):
        for w in range(3):
            g = gq_ref[...] if w == 0 else low[:, (w - 1) * cols : w * cols]
            product = mm_tn(s_ref[...], g)
            for half in range(halves):
                at = pl.multiple_of((w * halves + half) * depth + index * width, 128)
                gw_ref[pl.ds(at, width), :] = product[:, half * 128 : (half + 1) * 128]


def reduce_kernel(
    bits,
    gw_ref,
    gow_ref,
    taps_ref,
    gqw_ref,
    gkw_ref,
    gvw_ref,
    go_ref,
    taps_out_ref,
    acc,
    outgoing,
    incoming,
    final,
    taps_in,
    taps_sum,
    s_send,
    s_recv,
    g_send,
    g_recv,
    t_send,
    t_recv,
):
    me = lax.axis_index("slab")
    count = len(bits)
    span = acc.shape[0] // 2
    orders = (bits, bits[:1] + bits[2:] + bits[1:2])

    def bit_of(b):
        return lax.rem(lax.div(me, 1 << b), 2)

    def partner(b):
        return me + (1 - 2 * bit_of(b)) * (1 << b)

    barrier = pltpu.get_barrier_semaphore()
    for b in bits:
        pl.semaphore_signal(
            barrier, inc=1, device_id={"slab": partner(b)}, device_id_type=MESH
        )
    gw_rows = gw_ref.shape[0]
    acc[0:gw_rows, :] = gw_ref[...]
    acc[gw_rows:, :] = gow_ref[...]
    taps_sum[0] = taps_ref[...]
    pl.semaphore_wait(barrier, count)

    lows = [jnp.int32(0), jnp.int32(span)]
    trail = [[], []]
    waits = []
    size = span
    offset = 0
    for k in range(count):
        size //= 2
        copies = []
        for t in range(2):
            b = orders[t][k]
            bit = bit_of(b)
            keep = lows[t] + bit * size
            give = lows[t] + (1 - bit) * size
            slots = pl.ds(offset, size)
            outgoing[t, slots, :] = acc[pl.ds(pl.multiple_of(give, 16), size), :].astype(BF16)
            copy = pltpu.make_async_remote_copy(
                src_ref=outgoing.at[t, slots],
                dst_ref=incoming.at[t, slots],
                send_sem=s_send.at[t, k],
                recv_sem=s_recv.at[t, k],
                device_id={"slab": partner(b)},
                device_id_type=MESH,
            )
            copy.start()
            copies.append(copy)
            lows[t] = keep
            trail[t].append(keep)
        b = orders[0][k]
        taps_copy = pltpu.make_async_remote_copy(
            src_ref=taps_sum.at[k],
            dst_ref=taps_in.at[k],
            send_sem=t_send.at[k],
            recv_sem=t_recv.at[k],
            device_id={"slab": partner(b)},
            device_id_type=MESH,
        )
        taps_copy.start()
        for t in range(2):
            copies[t].wait_recv()
            at = pl.ds(pl.multiple_of(lows[t], 16), size)
            acc[at, :] = acc[at, :] + incoming[t, pl.ds(offset, size), :].astype(F32)
        taps_copy.wait_recv()
        taps_sum[k + 1] = taps_sum[k] + taps_in[k]
        waits += copies + [taps_copy]
        offset += size
    for t in range(2):
        at = pl.ds(pl.multiple_of(lows[t], 16), size)
        final[at, :] = acc[at, :].astype(BF16)
    for k in range(count - 1, -1, -1):
        copies = []
        for t in range(2):
            at = pl.ds(pl.multiple_of(trail[t][k], 16), size)
            copy = pltpu.make_async_remote_copy(
                src_ref=final.at[at],
                dst_ref=final.at[at],
                send_sem=g_send.at[t, k],
                recv_sem=g_recv.at[t, k],
                device_id={"slab": partner(orders[t][k])},
                device_id_type=MESH,
            )
            copy.start()
            copies.append(copy)
        for copy in copies:
            copy.wait_recv()
        waits += copies
        size *= 2
    for copy in waits:
        copy.wait_send()
    depth, cols = gqw_ref.shape
    at = 0
    for out in (gqw_ref, gkw_ref, gvw_ref, go_ref):
        rows = out.shape[0]
        for half in range(out.shape[1] // 128):
            out[:, half * 128 : (half + 1) * 128] = final[at : at + rows, :].astype(F32)
            at += rows
    taps_out_ref[...] = taps_sum[count]


def reduce_all(gw, gow, taps, depth, cols, slabs):
    rows = gw.shape[0] + gow.shape[0]
    bits = tuple(range(slabs.bit_length() - 1))
    count = len(bits)
    shapes = [jax.ShapeDtypeStruct((depth, cols), F32)] * 3
    shapes.append(jax.ShapeDtypeStruct((cols, depth), F32))
    shapes.append(jax.ShapeDtypeStruct(taps.shape, F32))
    dma = pltpu.SemaphoreType.DMA
    return pl.pallas_call(
        functools.partial(reduce_kernel, bits),
        out_shape=shapes,
        in_specs=[VMEM] * 3,
        out_specs=[VMEM] * 5,
        scratch_shapes=[
            pltpu.VMEM((rows, 128), F32),
            pltpu.VMEM((2, rows // 2, 128), BF16),
            pltpu.VMEM((2, rows // 2, 128), BF16),
            pltpu.VMEM((rows, 128), BF16),
            pltpu.VMEM((count,) + taps.shape, F32),
            pltpu.VMEM((count + 1,) + taps.shape, F32),
            dma((2, count)),
            dma((2, count)),
            dma((2, count)),
            dma((2, count)),
            dma((count,)),
            dma((count,)),
        ],
        compiler_params=pltpu.CompilerParams(
            collective_id=0, has_side_effects=True, vmem_limit_bytes=LIMIT
        ),
    )(gw, gow, taps)


def body(
    slabs,
    tokens,
    stem_taps,
    query_weight,
    key_weight,
    value_weight,
    out_weight,
    key_blocks,
    counts,
    cotangent,
):
    count, width = tokens.shape
    depth, cols = query_weight.shape
    plane = PLANE_TOK
    sds = jax.ShapeDtypeStruct
    params = pltpu.CompilerParams(vmem_limit_bytes=LIMIT)
    up = [(i, (i + 1) % slabs) for i in range(slabs)]
    down = [(i, (i - 1) % slabs) for i in range(slabs)]

    def to_next(x):
        return lax.ppermute(x, "slab", up)

    def to_prev(x):
        return lax.ppermute(x, "slab", down)

    def swap(x):
        return lax.ppermute(x, "tp", [(0, 1), (1, 0)])

    before = jnp.concatenate([to_next(tokens[count - plane :]), tokens[: count - plane]])
    after = jnp.concatenate([tokens[plane:], to_prev(tokens[:plane])])
    before_f, own_f, after_f = before.astype(F32), tokens.astype(F32), after.astype(F32)
    stem = (stem_taps[0] * before_f + stem_taps[1] * own_f + stem_taps[2] * after_f).astype(BF16)
    stem_other = swap(stem)
    cot_other = swap(cotangent)

    q, kv = pl.pallas_call(
        project_kernel,
        out_shape=[sds((count, cols), BF16), sds((count, 2 * cols), BF16)],
        in_specs=[VMEM] * 5,
        out_specs=[VMEM] * 2,
        compiler_params=params,
    )(stem, stem_other, query_weight, key_weight, value_weight)
    kv_prev = to_next(kv[count - plane :])
    kv_next = to_prev(kv[:plane])

    gq, gkv, gprev, gnext, mix, mix_other, gow = pl.pallas_call(
        functools.partial(attention_kernel, slabs),
        out_shape=[
            sds((count, cols), BF16),
            sds((count, 2 * cols), F32),
            sds((plane, 2 * cols), BF16),
            sds((plane, 2 * cols), BF16),
            sds((count, width), F32),
            sds((count, width), BF16),
            sds((cols * depth // 128, 128), F32),
        ],
        in_specs=[SMEM, SMEM, VMEM, ANY, ANY, ANY, VMEM, VMEM, VMEM],
        out_specs=[VMEM] * 7,
        scratch_shapes=[
            pltpu.VMEM((count + 2 * plane, 2 * cols), BF16),
            pltpu.VMEM((count + 2 * plane, 2 * cols), F32),
            pltpu.VMEM((count, cols), BF16),
            pltpu.VMEM((count, cols), BF16),
            pltpu.SemaphoreType.DMA((3,)),
        ],
        compiler_params=params,
    )(key_blocks, counts, q, kv, kv_prev, kv_next, cotangent, cot_other, out_weight)
    from_next = to_prev(gprev)
    from_prev = to_next(gnext)
    layer_out = (stem.astype(F32) + (mix + swap(mix_other).astype(F32))).astype(BF16)

    own, other, gw = pl.pallas_call(
        gradient_kernel,
        out_shape=[
            sds((count, width), F32),
            sds((count, width), BF16),
            sds((3 * depth * cols // 128, 128), F32),
        ],
        in_specs=[VMEM] * 9,
        out_specs=[VMEM] * 3,
        scratch_shapes=[pltpu.VMEM((count, 2 * cols), BF16)],
        compiler_params=params,
    )(gq, gkv, from_prev, from_next, stem, stem_other, query_weight, key_weight, value_weight)

    grad_stem = cotangent.astype(F32) + (own + swap(other).astype(F32))
    grad_low = grad_stem.astype(BF16)
    grad_prev = to_next(grad_low[count - plane :]).astype(F32)
    grad_next = to_prev(grad_low[:plane]).astype(F32)
    grad_after = jnp.concatenate([grad_stem[plane:], grad_next])
    grad_before = jnp.concatenate([grad_prev, grad_stem[: count - plane]])
    grad_tokens = (
        stem_taps[0] * grad_after + stem_taps[1] * grad_stem + stem_taps[2] * grad_before
    )
    taps = jnp.stack([jnp.sum(grad_stem * x, axis=0) for x in (before_f, own_f, after_f)])
    gqw, gkw, gvw, go, grad_taps = reduce_all(gw, gow, taps, depth, cols, slabs)
    return (layer_out, grad_tokens, grad_taps, gqw, gkw, gvw, go)


def solution(mesh):
    in_specs = (
        P("slab", "tp"),
        P(None, "tp"),
        P(None, "tp"),
        P(None, "tp"),
        P(None, "tp"),
        P("tp", None),
        P("slab", None),
        P("slab"),
        P("slab", "tp"),
    )
    out_specs = (
        P("slab", "tp"),
        P("slab", "tp"),
        P(None, "tp"),
        P(None, "tp"),
        P(None, "tp"),
        P(None, "tp"),
        P("tp", None),
    )
    return jax.shard_map(
        functools.partial(body, mesh.shape["slab"]),
        mesh=mesh,
        in_specs=in_specs,
        out_specs=out_specs,
        check_vma=False,
    )
```

time: 521 us -> 154 us (0.30); the launches traced: 512 us -> 153 us
  matrix products: 119 us -> 0 us
  local copies, waits for them, and re-layouts: 119 us -> 11.3 us
  waiting for transfers between devices: 133 us -> 45.2 us
  Pallas kernels: 0 us -> 66 us
  other arithmetic: 65.1 us -> 4.74 us
  blocking collectives: 34.2 us -> 0 us
  between operations: 14.3 us -> 0.78 us
  loops' own time: 8.71 us -> 0 us
  starting transfers between devices: 18.5 us -> 25.1 us
    dot_general x24 -> x0, matrix products: 110 us -> none  [the longest x2 37.9 us: backward_group(): jnp.einsum('ghqk,gqhd->gkhd', grad_scores, query_block, preferred_element...]
    pallas_call x0 -> x4, Pallas kernels: none -> 66 us  [the longest x1 36 us: reduce_all(): pl.pallas_call(functools.partial(reduce_kernel, bits), out_shape=shapes,...]
    psum x1 -> x0, waiting for transfers between devices: 63.4 us -> none  [body(): lax.psum((grad_query_weight, grad_key_weight, grad_value_weight, grad_out...]
    all_gather x2 -> x0, waiting for transfers between devices: 35.9 us -> none  [the longest x1 22 us: body(): lax.all_gather(stem_own, 'tp', axis=1, tiled=True)]
    gather x8 -> x0, local copies, waits for them, and re-layouts: 35.1 us -> none  [fetch(): picked = jnp.take(table, block_ids.reshape(-1), axis=0)]
    psum x1 -> x0, blocking collectives: 34.2 us -> none  [body(): lax.psum((grad_query_weight, grad_key_weight, grad_value_weight, grad_out...]
    ppermute x8 -> x12, waiting for transfers between devices: 12.6 us -> 45.2 us  [the longest x4 21.5 us: swap(): return lax.ppermute(x, 'tp', [(0, 1), (1, 0)])]
    another operation x10 -> x0, local copies, waits for them, and re-layouts: 30.1 us -> none  [the longest x6 23.1 us: backward_group(): jnp.stack([grad_key, grad_value]).reshape(2, 4 * MAXK, BLK, head_cols)]
  transfers between devices with their start and end apart: 13 -> 12, of which waited for: 7 -> 7; matrix products, arithmetic and copies ran while one was open for 14% -> 3% of each run, Pallas kernels for 0% -> 7%
where the time goes in v1:
time: 154 us; the launch traced here: 153 us
  Pallas kernels  66 us (43%)
  waiting for transfers between devices  45.2 us (29%)
  starting transfers between devices  25.1 us (16%)
  local copies, waits for them, and re-layouts  11.3 us (7%)
  other arithmetic  4.74 us (3%)
    pallas_call x1, Pallas kernels, reduce_all(): pl.pallas_call(functools.partial(reduce_kernel, bits), out_shape=shapes,...  36 us
    ppermute x4, waiting for transfers between devices, swap(): return lax.ppermute(x, 'tp', [(0, 1), (1, 0)])  21.5 us
    pallas_call x1, Pallas kernels, body(): pl.pallas_call(functools.partial(attention_kernel, slabs), out_shape=[sds...  19.5 us
    ppermute x4, starting transfers between devices, to_prev(): return lax.ppermute(x, 'slab', down)  17.9 us
    ppermute x4, waiting for transfers between devices, to_next(): return lax.ppermute(x, 'slab', up)  17.4 us
    unnamed x44, local copies, waits for them, and re-layouts  7.04 us
    pallas_call x1, Pallas kernels, body(): pl.pallas_call(gradient_kernel, out_shape=[sds((count, width), F32), sds(...  6.56 us
    ppermute x4, waiting for transfers between devices, to_prev(): return lax.ppermute(x, 'slab', down)  6.34 us
  transfers between devices with their start and end apart: 12, of which 7 were waited for; matrix products, arithmetic and copies ran while one was open for 3% of the time, Pallas kernels for 7%

profile of v1, /device:TPU:0, one launch (start us, length us, event | category | flops | bytes accessed | tf_op | source)
XLA Modules:
  0.0 153.2 jit_solution(3217065644102331328)
XLA Ops:
  0.6 1.1 fusion.11
  2.3 5.0 %collective-permute-start.1 = (bf16[512,256]{1,0:T(8,128)(2,1)S(1)}, bf16[512,256]{1,0:T(8,128)(2,1)S(1)}, u32[]{:S(2)}, u32[]{:S(2)}) collective-permute-start(bf16[512,256]{1,0:T(8,128)(2,1)S(1)} %get-tuple-element.52), channel_id=1, source_target_pairs={{0,30},{2,0},{4,2},{6,4},{8,6},{10,8},{12,10},{14,12},{16,14},{18,... | collective-permute-start | bytes 786440 | tf_op jit(solution)/shard_map/ppermute | solution.py:416
  7.3 0.8 fusion.12
  8.1 3.3 %collective-permute-done = bf16[512,256]{1,0:T(8,128)(2,1)S(1)} collective-permute-done((bf16[512,256]{1,0:T(8,128)(2,1)S(1)}, bf16[512,256]{1,0:T(8,128)(2,1)S(1)}, u32[]{:S(2)}, u32[]{:S(2)}) %collective-permute-start) | collective-permute-done | bytes 262176 | tf_op jit(solution)/shard_map/ppermute | solution.py:413
  11.4 1.3 fusion.2.so_ref
  12.8 2.1 %collective-permute-start.2 = (bf16[1024,256]{1,0:T(8,128)(2,1)S(1)}, bf16[1024,256]{1,0:T(8,128)(2,1)S(1)}, u32[]{:S(2)}, u32[]{:S(2)}) collective-permute-start(bf16[1024,256]{1,0:T(8,128)(2,1)S(1)} %fusion.2.so_ref), channel_id=1, source_target_pairs={{0,1},{1,0},{2,3},{3,2},{4,5},{5,4},{6,7},{7,6},{8,9},{9,8},{10,11... | collective-permute-start | bytes 1572872 | tf_op jit(solution)/shard_map/ppermute | solution.py:419
  14.9 11.6 %collective-permute-done.2.st_ref = bf16[1024,256]{1,0:T(8,128)(2,1)S(1)} collective-permute-done((bf16[1024,256]{1,0:T(8,128)(2,1)S(1)}, bf16[1024,256]{1,0:T(8,128)(2,1)S(1)}, u32[]{:S(2)}, u32[]{:S(2)}) %collective-permute-start.2) | collective-permute-done | bytes 524320 | tf_op jit(solution)/shard_map/ppermute | solution.py:419
  26.5 0.8 copy-done.5
  27.3 3.9 %shard_map.144 = (bf16[1024,256]{1,0:T(8,128)(2,1)}, bf16[1024,512]{1,0:T(8,128)(2,1)}) custom-call(bf16[1024,256]{1,0:T(8,128)(2,1)} %copy-done, bf16[1024,256]{1,0:T(8,128)(2,1)} %copy-done.5, bf16[512,256]{1,0:T(8,128)(2,1)} %wq_ref.3, bf16[512,256]{1,0:T(8,128)(2,1)} %wk_ref.3, bf16[512,256]{1,0:T(8,128)(2,1)} %wv_ref.3), custom_call_target="tpu_custom_call" | custom-call | tf_op jit(solution)/shard_map/pallas_call | solution.py:428
  31.3 2.2 %fusion.9 = (bf16[512,512]{1,0:T(8,128)(2,1)}, bf16[512,512]{1,0:T(8,128)(2,1)}) fusion(bf16[1024,512]{1,0:T(8,128)(2,1)} %get-tuple-element.25.kv_ref), kind=kLoop, calls=%fused_computation.22 | loop fusion | bytes 2097152 | tf_op jit(solution)/shard_map/slice | solution.py:436
  33.5 4.8 %collective-permute-start.4 = (bf16[512,512]{1,0:T(8,128)(2,1)}, bf16[512,512]{1,0:T(8,128)(2,1)S(1)}, u32[]{:S(2)}, u32[]{:S(2)}) collective-permute-start(bf16[512,512]{1,0:T(8,128)(2,1)} %get-tuple-element.47), channel_id=1, source_target_pairs={{0,30},{2,0},{4,2},{6,4},{8,6},{10,8},{12,10},{14,12},{16,14},{18,... | collective-permute-start | bytes 1572872 | tf_op jit(solution)/shard_map/ppermute | solution.py:416
  38.3 0.7 copy.16.blocks_ref
  39.0 6.3 %collective-permute-done.4.kv_next_ref = bf16[512,512]{1,0:T(8,128)(2,1)S(1)} collective-permute-done((bf16[512,512]{1,0:T(8,128)(2,1)}, bf16[512,512]{1,0:T(8,128)(2,1)S(1)}, u32[]{:S(2)}, u32[]{:S(2)}) %collective-permute-start.4) | collective-permute-done | bytes 524320 | tf_op jit(solution)/shard_map/ppermute | solution.py:416
  45.4 4.6 %collective-permute-done.3.kv_prev_ref = bf16[512,512]{1,0:T(8,128)(2,1)S(1)} collective-permute-done((bf16[512,512]{1,0:T(8,128)(2,1)}, bf16[512,512]{1,0:T(8,128)(2,1)S(1)}, u32[]{:S(2)}, u32[]{:S(2)}) %collective-permute-start.3) | collective-permute-done | bytes 524320 | tf_op jit(solution)/shard_map/ppermute | solution.py:413
  50.0 0.8 copy-done.10
  50.7 19.5 %shard_map.145 = (bf16[1024,256]{1,0:T(8,128)(2,1)}, f32[1024,512]{1,0:T(8,128)}, bf16[512,512]{1,0:T(8,128)(2,1)}, bf16[512,512]{1,0:T(8,128)(2,1)}, f32[1024,2...) custom-call(s32[8,4]{1,0:T(8,128)} %copy.16.blocks_ref, s32[8]{0:T(128)} %counts_ref.1, ...), custom_call_target="tpu_custom_call" | custom-call | tf_op jit(solution)/shard_map/pallas_call | solution.py:438
  70.8 4.0 %collective-permute-start.8 = (bf16[512,512]{1,0:T(8,128)(2,1)}, bf16[512,512]{1,0:T(8,128)(2,1)S(1)}, u32[]{:S(2)}, u32[]{:S(2)}) collective-permute-start(bf16[512,512]{1,0:T(8,128)(2,1)} %get-tuple-element.31), channel_id=1, source_target_pairs={{0,30},{2,0},{4,2},{6,4},{8,6},{10,8},{12,10},{14,12},{16,14},{18,... | collective-permute-start | bytes 1572872 | tf_op jit(solution)/shard_map/ppermute | solution.py:416
  74.8 1.7 %collective-permute-start.6 = (bf16[1024,256]{1,0:T(8,128)(2,1)}, bf16[1024,256]{1,0:T(8,128)(2,1)S(1)}, u32[]{:S(2)}, u32[]{:S(2)}) collective-permute-start(bf16[1024,256]{1,0:T(8,128)(2,1)} %get-tuple-element.27), channel_id=1, source_target_pairs={{0,1},{1,0},{2,3},{3,2},{4,5},{5,4},{6,7},{7,6},{8,9},{9,8},{10,11... | collective-permute-start | bytes 1572872 | tf_op jit(solution)/shard_map/ppermute | solution.py:419
  76.5 5.4 %collective-permute-done.7.from_prev_ref = bf16[512,512]{1,0:T(8,128)(2,1)S(1)} collective-permute-done((bf16[512,512]{1,0:T(8,128)(2,1)}, bf16[512,512]{1,0:T(8,128)(2,1)S(1)}, u32[]{:S(2)}, u32[]{:S(2)}) %collective-permute-start.7) | collective-permute-done | bytes 524320 | tf_op jit(solution)/shard_map/ppermute | solution.py:413
  82.0 0.8 copy-done.16
  82.9 6.6 %shard_map.146 = (f32[1024,256]{1,0:T(8,128)}, bf16[1024,256]{1,0:T(8,128)(2,1)}, f32[3072,128]{1,0:T(8,128)}) custom-call(bf16[1024,256]{1,0:T(8,128)(2,1)} %get-tuple-element.28.gq_ref, f32[1024,512]{1,0:T(8,128)} %get-tuple-element.29.gkv_ref, bf16[512,512]{1,0:T(8,128)(2,1)} %copy-done.15, bf16[512,512]{1,0:T(8,128)(2,1)} %copy-done.16, ...), custom_call_target="tpu_custom_call" | custom-call | tf_op jit(solution)/shard_map/pallas_call | solution.py:464
  89.5 1.8 %collective-permute-start.9 = (bf16[1024,256]{1,0:T(8,128)(2,1)}, bf16[1024,256]{1,0:T(8,128)(2,1)S(1)}, u32[]{:S(2)}, u32[]{:S(2)}) collective-permute-start(bf16[1024,256]{1,0:T(8,128)(2,1)} %get-tuple-element.33), channel_id=1, source_target_pairs={{0,1},{1,0},{2,3},{3,2},{4,5},{5,4},{6,7},{7,6},{8,9},{9,8},{10,11... | collective-permute-start | bytes 1572872 | tf_op jit(solution)/shard_map/ppermute | solution.py:419
  91.3 1.0 add_convert_fusion
  92.3 9.9 %collective-permute-done.9 = bf16[1024,256]{1,0:T(8,128)(2,1)S(1)} collective-permute-done((bf16[1024,256]{1,0:T(8,128)(2,1)}, bf16[1024,256]{1,0:T(8,128)(2,1)S(1)}, u32[]{:S(2)}, u32[]{:S(2)}) %collective-permute-start.9) | collective-permute-done | bytes 524320 | tf_op jit(solution)/shard_map/ppermute | solution.py:419
  103.3 36.0 %shard_map.147 = (f32[512,256]{1,0:T(8,128)}, f32[512,256]{1,0:T(8,128)}, f32[512,256]{1,0:T(8,128)}, f32[256,512]{1,0:T(8,128)}, f32[3,256]{1,0:T(4,128)}) custom-call(f32[3072,128]{1,0:T(8,128)} %get-tuple-element.34.gw_ref, f32[1024,128]{1,0:T(8,128)} %get-tuple-element.35.gow_ref, f32[3,256]{1,0:T(4,128)} %pad_maximum_fusion.2.taps_ref), custom_call_target="tpu_custom_call" | custom-call | tf_op jit(solution)/shard_map/pallas_call | solution.py:367
  139.9 4.0 %collective-permute-start.10 = (bf16[512,256]{1,0:T(8,128)(2,1)S(1)}, bf16[512,256]{1,0:T(8,128)(2,1)S(1)}, u32[]{:S(2)}, u32[]{:S(2)}) collective-permute-start(bf16[512,256]{1,0:T(8,128)(2,1)S(1)} %get-tuple-element.50), channel_id=1, source_target_pairs={{0,30},{2,0},{4,2},{6,4},{8,6},{10,8},{12,10},{14,12},{16,14},{18,... | collective-permute-start | bytes 786440 | tf_op jit(solution)/shard_map/ppermute | solution.py:416
  144.0 4.1 %collective-permute-done.11 = bf16[512,256]{1,0:T(8,128)(2,1)S(1)} collective-permute-done((bf16[512,256]{1,0:T(8,128)(2,1)S(1)}, bf16[512,256]{1,0:T(8,128)(2,1)S(1)}, u32[]{:S(2)}, u32[]{:S(2)}) %collective-permute-start.11) | collective-permute-done | bytes 262176 | tf_op jit(solution)/shard_map/ppermute | solution.py:413
  148.2 1.2 fusion.7
  150.0 0.8 copy.23
  150.8 0.8 copy.24
  151.6 0.8 copy.25
  152.4 0.8 copy.26
  (53 shorter events, 3.8 us)
Async XLA Ops:
  0.6 14.2 %copy-start.3 = (bf16[1024,256]{1,0:T(8,128)(2,1)S(1)}, bf16[1024,256]{1,0:T(8,128)(2,1)}, u32[]{:S(2)}) copy-start(bf16[1024,256]{1,0:T(8,128)(2,1)} %co_ref.1) | copy-start | bytes 1572868
  1.8 9.7 %collective-permute-start = (bf16[512,256]{1,0:T(8,128)(2,1)S(1)}, bf16[512,256]{1,0:T(8,128)(2,1)S(1)}, u32[]{:S(2)}, u32[]{:S(2)}) collective-permute-start(bf16[512,256]{1,0:T(8,128)(2,1)S(1)} %get-tuple-element.51), channel_id=1, source_target_pairs={{0,2},{2,4},{4,6},{6,8},{8,10},{10,12},{12,14},{14,16},{16,18},{18... | collective-permute-start | bytes 786440 | tf_op jit(solution)/shard_map/ppermute | solution.py:413
  2.3 9.1 %collective-permute-start.1 = (bf16[512,256]{1,0:T(8,128)(2,1)S(1)}, bf16[512,256]{1,0:T(8,128)(2,1)S(1)}, u32[]{:S(2)}, u32[]{:S(2)}) collective-permute-start(bf16[512,256]{1,0:T(8,128)(2,1)S(1)} %get-tuple-element.52), channel_id=1, source_target_pairs={{0,30},{2,0},{4,2},{6,4},{8,6},{10,8},{12,10},{14,12},{16,14},{18,... | collective-permute-start | bytes 786440 | tf_op jit(solution)/shard_map/ppermute | solution.py:416
  12.8 13.8 %copy-start = (bf16[1024,256]{1,0:T(8,128)(2,1)}, bf16[1024,256]{1,0:T(8,128)(2,1)S(1)}, u32[]{:S(2)}) copy-start(bf16[1024,256]{1,0:T(8,128)(2,1)S(1)} %fusion.2.so_ref) | copy-start | bytes 1572868
  12.8 25.6 %copy-start.18 = (s32[8,4]{0,1:T(4,128)S(1)}, s32[8,4]{0,1:T(4,128)}, u32[]{:S(2)}) copy-start(s32[8,4]{0,1:T(4,128)} %param.15) | copy-start | bytes 388
  12.8 13.8 %collective-permute-start.2 = (bf16[1024,256]{1,0:T(8,128)(2,1)S(1)}, bf16[1024,256]{1,0:T(8,128)(2,1)S(1)}, u32[]{:S(2)}, u32[]{:S(2)}) collective-permute-start(bf16[1024,256]{1,0:T(8,128)(2,1)S(1)} %fusion.2.so_ref), channel_id=1, source_target_pairs={{0,1},{1,0},{2,3},{3,2},{4,5},{5,4},{6,7},{7,6},{8,9},{9,8},{10,11... | collective-permute-start | bytes 1572872 | tf_op jit(solution)/shard_map/ppermute | solution.py:419
  14.8 24.2 %collective-permute-start.5 = (bf16[1024,256]{1,0:T(8,128)(2,1)S(1)}, bf16[1024,256]{1,0:T(8,128)(2,1)S(1)}, u32[]{:S(2)}, u32[]{:S(2)}) collective-permute-start(bf16[1024,256]{1,0:T(8,128)(2,1)S(1)} %copy-done.3), channel_id=1, source_target_pairs={{0,1},{1,0},{2,3},{3,2},{4,5},{5,4},{6,7},{7,6},{8,9},{9,8},{10,11... | collective-permute-start | bytes 1572872 | tf_op jit(solution)/shard_map/ppermute | solution.py:419
  26.5 0.8 copy-start.5
  33.5 11.9 %collective-permute-start.4 = (bf16[512,512]{1,0:T(8,128)(2,1)}, bf16[512,512]{1,0:T(8,128)(2,1)S(1)}, u32[]{:S(2)}, u32[]{:S(2)}) collective-permute-start(bf16[512,512]{1,0:T(8,128)(2,1)} %get-tuple-element.47), channel_id=1, source_target_pairs={{0,30},{2,0},{4,2},{6,4},{8,6},{10,8},{12,10},{14,12},{16,14},{18,... | collective-permute-start | bytes 1572872 | tf_op jit(solution)/shard_map/ppermute | solution.py:416
  38.3 11.6 %collective-permute-start.3 = (bf16[512,512]{1,0:T(8,128)(2,1)}, bf16[512,512]{1,0:T(8,128)(2,1)S(1)}, u32[]{:S(2)}, u32[]{:S(2)}) collective-permute-start(bf16[512,512]{1,0:T(8,128)(2,1)} %get-tuple-element.48), channel_id=1, source_target_pairs={{0,2},{2,4},{4,6},{6,8},{8,10},{10,12},{12,14},{14,16},{16,18},{18... | collective-permute-start | bytes 1572872 | tf_op jit(solution)/shard_map/ppermute | solution.py:413
  39.0 10.9 %copy-start.8 = (bf16[1024,256]{1,0:T(8,128)(2,1)}, bf16[1024,256]{1,0:T(8,128)(2,1)S(1)}, u32[]{:S(2)}) copy-start(bf16[1024,256]{1,0:T(8,128)(2,1)S(1)} %collective-permute-done.5.ct_ref) | copy-start | bytes 1572868
  45.4 4.6 %copy-start.9 = (bf16[512,512]{1,0:T(8,128)(2,1)}, bf16[512,512]{1,0:T(8,128)(2,1)S(1)}, u32[]{:S(2)}) copy-start(bf16[512,512]{1,0:T(8,128)(2,1)S(1)} %collective-permute-done.4.kv_next_ref) | copy-start | bytes 1572868
  50.0 0.8 copy-start.10
  70.3 11.7 %collective-permute-start.7 = (bf16[512,512]{1,0:T(8,128)(2,1)}, bf16[512,512]{1,0:T(8,128)(2,1)S(1)}, u32[]{:S(2)}, u32[]{:S(2)}) collective-permute-start(bf16[512,512]{1,0:T(8,128)(2,1)} %get-tuple-element.30), channel_id=1, source_target_pairs={{0,2},{2,4},{4,6},{6,8},{8,10},{10,12},{12,14},{14,16},{16,18},{18... | collective-permute-start | bytes 1572872 | tf_op jit(solution)/shard_map/ppermute | solution.py:413
  70.8 11.1 %collective-permute-start.8 = (bf16[512,512]{1,0:T(8,128)(2,1)}, bf16[512,512]{1,0:T(8,128)(2,1)S(1)}, u32[]{:S(2)}, u32[]{:S(2)}) collective-permute-start(bf16[512,512]{1,0:T(8,128)(2,1)} %get-tuple-element.31), channel_id=1, source_target_pairs={{0,30},{2,0},{4,2},{6,4},{8,6},{10,8},{12,10},{14,12},{16,14},{18,... | collective-permute-start | bytes 1572872 | tf_op jit(solution)/shard_map/ppermute | solution.py:416
  74.8 16.5 %collective-permute-start.6 = (bf16[1024,256]{1,0:T(8,128)(2,1)}, bf16[1024,256]{1,0:T(8,128)(2,1)S(1)}, u32[]{:S(2)}, u32[]{:S(2)}) collective-permute-start(bf16[1024,256]{1,0:T(8,128)(2,1)} %get-tuple-element.27), channel_id=1, source_target_pairs={{0,1},{1,0},{2,3},{3,2},{4,5},{5,4},{6,7},{7,6},{8,9},{9,8},{10,11... | collective-permute-start | bytes 1572872 | tf_op jit(solution)/shard_map/ppermute | solution.py:419
  82.0 1.0 copy-start.15
  82.0 0.8 copy-start.16
  82.9 8.4 %copy-start.1 = (bf16[1024,256]{1,0:T(8,128)(2,1)S(1)}, bf16[1024,256]{1,0:T(8,128)(2,1)}, u32[]{:S(2)}) copy-start(bf16[1024,256]{1,0:T(8,128)(2,1)} %copy-done) | copy-start | bytes 1572868
  82.9 8.4 %copy-start.7 = (f32[1024,256]{1,0:T(8,128)S(1)}, f32[1024,256]{1,0:T(8,128)}, u32[]{:S(2)}) copy-start(f32[1024,256]{1,0:T(8,128)} %get-tuple-element.26) | copy-start | bytes 3145732
  89.5 12.7 %copy-start.2 = (bf16[1024,256]{1,0:T(8,128)(2,1)S(1)}, bf16[1024,256]{1,0:T(8,128)(2,1)}, u32[]{:S(2)}) copy-start(bf16[1024,256]{1,0:T(8,128)(2,1)} %param.9) | copy-start | bytes 1572868
  89.5 12.7 %copy-start.4 = (bf16[1024,256]{1,0:T(8,128)(2,1)S(1)}, bf16[1024,256]{1,0:T(8,128)(2,1)}, u32[]{:S(2)}) copy-start(bf16[1024,256]{1,0:T(8,128)(2,1)} %co_ref.1) | copy-start | bytes 1572868
  89.5 12.7 %copy-start.6 = (f32[1024,256]{1,0:T(8,128)S(1)}, f32[1024,256]{1,0:T(8,128)}, u32[]{:S(2)}) copy-start(f32[1024,256]{1,0:T(8,128)} %get-tuple-element.32) | copy-start | bytes 3145732
  89.5 12.7 %collective-permute-start.9 = (bf16[1024,256]{1,0:T(8,128)(2,1)}, bf16[1024,256]{1,0:T(8,128)(2,1)S(1)}, u32[]{:S(2)}, u32[]{:S(2)}) collective-permute-start(bf16[1024,256]{1,0:T(8,128)(2,1)} %get-tuple-element.33), channel_id=1, source_target_pairs={{0,1},{1,0},{2,3},{3,2},{4,5},{5,4},{6,7},{7,6},{8,9},{9,8},{10,11... | collective-permute-start | bytes 1572872 | tf_op jit(solution)/shard_map/ppermute | solution.py:419
  139.4 8.7 %collective-permute-start.11 = (bf16[512,256]{1,0:T(8,128)(2,1)S(1)}, bf16[512,256]{1,0:T(8,128)(2,1)S(1)}, u32[]{:S(2)}, u32[]{:S(2)}) collective-permute-start(bf16[512,256]{1,0:T(8,128)(2,1)S(1)} %get-tuple-element.49), channel_id=1, source_target_pairs={{0,2},{2,4},{4,6},{6,8},{8,10},{10,12},{12,14},{14,16},{16,18},{18... | collective-permute-start | bytes 786440 | tf_op jit(solution)/shard_map/ppermute | solution.py:413
  139.9 8.2 %collective-permute-start.10 = (bf16[512,256]{1,0:T(8,128)(2,1)S(1)}, bf16[512,256]{1,0:T(8,128)(2,1)S(1)}, u32[]{:S(2)}, u32[]{:S(2)}) collective-permute-start(bf16[512,256]{1,0:T(8,128)(2,1)S(1)} %get-tuple-element.50), channel_id=1, source_target_pairs={{0,30},{2,0},{4,2},{6,4},{8,6},{10,8},{12,10},{14,12},{16,14},{18,... | collective-permute-start | bytes 786440 | tf_op jit(solution)/shard_map/ppermute | solution.py:416
  148.2 1.2 copy-start.17
  148.2 1.8 %copy-start.14 = (f32[512,256]{1,0:T(8,128)S(1)}, f32[512,256]{1,0:T(8,128)}, u32[]{:S(2)}) copy-start(f32[512,256]{1,0:T(8,128)} %get-tuple-element.66) | copy-start | bytes 1572868
  148.2 2.6 %copy-start.13 = (f32[512,256]{1,0:T(8,128)S(1)}, f32[512,256]{1,0:T(8,128)}, u32[]{:S(2)}) copy-start(f32[512,256]{1,0:T(8,128)} %get-tuple-element.67) | copy-start | bytes 1572868
  149.4 2.2 %copy-start.12 = (f32[512,256]{1,0:T(8,128)S(1)}, f32[512,256]{1,0:T(8,128)}, u32[]{:S(2)}) copy-start(f32[512,256]{1,0:T(8,128)} %get-tuple-element.68) | copy-start | bytes 1572868
  149.4 3.0 %copy-start.11 = (f32[256,512]{1,0:T(8,128)S(1)}, f32[256,512]{1,0:T(8,128)}, u32[]{:S(2)}) copy-start(f32[256,512]{1,0:T(8,128)} %get-tuple-element.69) | copy-start | bytes 1572868

commit v2 on v1

--- a/solution.py
+++ b/solution.py
@@ -176,217 +176,306 @@
             ]
 
 
-def gradient_kernel(
+def copy_to(src, dst, send, recv, where):
+    return pltpu.make_async_remote_copy(
+        src_ref=src,
+        dst_ref=dst,
+        send_sem=send,
+        recv_sem=recv,
+        device_id=where,
+        device_id_type=MESH,
+    )
+
+
+def backward_kernel(
+    slabs,
     gq_ref,
     gkv_ref,
-    from_prev_ref,
-    from_next_ref,
+    gprev_ref,
+    gnext_ref,
     so_ref,
     st_ref,
     wq_ref,
     wk_ref,
     wv_ref,
-    part_ref,
-    part_other_ref,
-    gw_ref,
+    gow_ref,
+    mix_ref,
+    mix_other_ref,
+    cot_ref,
+    tok_ref,
+    tok_prev_ref,
+    tok_next_ref,
+    taps_ref,
+    layer_ref,
+    grad_ref,
+    final,
+    taps_out_ref,
     low,
-):
-    tp = lax.axis_index("tp")
-    tokens, cols = gq_ref.shape
-    width = so_ref.shape[1]
-    depth = wq_ref.shape[0]
-    mine, other = part(tp, width), part(1 - tp, width)
-    low[...] = gkv_ref[...].astype(BF16)
-    last = tokens - PLANE_TOK
-    if last > 0:
-        low[0:PLANE_TOK, :] = (gkv_ref[0:PLANE_TOK, :] + from_prev_ref[...].astype(F32)).astype(
-            BF16
-        )
-        low[last:, :] = (gkv_ref[last:, :] + from_next_ref[...].astype(F32)).astype(BF16)
-    else:
-        low[...] = (
-            gkv_ref[...] + from_prev_ref[...].astype(F32) + from_next_ref[...].astype(F32)
-        ).astype(BF16)
-
-    @pl.loop(0, tokens // CHUNK)
-    def _(step):
-        rows = part(step, CHUNK)
-        gq = gq_ref[rows, :]
-        gk = low[rows, 0:cols]
-        gv = low[rows, cols : 2 * cols]
-
-        def back(at):
-            return (
-                mm_nt(gq, wq_ref[at, :]) + mm_nt(gk, wk_ref[at, :]) + mm_nt(gv, wv_ref[at, :])
-            )
-
-        part_ref[rows, :] = back(mine)
-        part_other_ref[rows, :] = back(other).astype(BF16)
-
-    halves = cols // 128
-    for index, s_ref in ((tp, so_ref), (1 - tp, st_ref)):
-        for w in range(3):
-            g = gq_ref[...] if w == 0 else low[:, (w - 1) * cols : w * cols]
-            product = mm_tn(s_ref[...], g)
-            for half in range(halves):
-                at = pl.multiple_of((w * halves + half) * depth + index * width, 128)
-                gw_ref[pl.ds(at, width), :] = product[:, half * 128 : (half + 1) * 128]
-
-
-def reduce_kernel(
-    bits,
-    gw_ref,
-    gow_ref,
-    taps_ref,
-    gqw_ref,
-    gkw_ref,
-    gvw_ref,
-    go_ref,
-    taps_out_ref,
+    from_prev,
+    from_next,
+    mix_in,
+    own,
+    other,
+    part_out,
+    part_in,
+    edge,
+    edge_prev,
+    edge_next,
     acc,
     outgoing,
     incoming,
-    final,
     taps_in,
     taps_sum,
+    h_send,
+    h_recv,
+    m_send,
+    m_recv,
+    p_send,
+    p_recv,
+    e_send,
+    e_recv,
     s_send,
     s_recv,
-    g_send,
-    g_recv,
     t_send,
     t_recv,
 ):
     me = lax.axis_index("slab")
-    count = len(bits)
+    tp = lax.axis_index("tp")
+    bits = tuple(range(slabs.bit_length() - 1))
+    stages = len(bits)
+    orders = (bits, bits[:1] + bits[2:] + bits[1:2])
+    tokens, cols = gq_ref.shape
+    width = so_ref.shape[1]
+    depth = wq_ref.shape[0]
+    halves = cols // 128
     span = acc.shape[0] // 2
-    orders = (bits, bits[:1] + bits[2:] + bits[1:2])
+    last = tokens - PLANE_TOK
+    chunks = tokens // CHUNK
+    edge_chunks = PLANE_TOK // CHUNK
+    mine, theirs = part(tp, width), part(1 - tp, width)
+    nxt = {"slab": lax.rem(me + 1, slabs)}
+    prv = {"slab": lax.rem(me + slabs - 1, slabs)}
+    mate = {"tp": 1 - tp}
 
     def bit_of(b):
         return lax.rem(lax.div(me, 1 << b), 2)
 
     def partner(b):
-        return me + (1 - 2 * bit_of(b)) * (1 << b)
+        return {"slab": me + (1 - 2 * bit_of(b)) * (1 << b)}
 
     barrier = pltpu.get_barrier_semaphore()
-    for b in bits:
-        pl.semaphore_signal(
-            barrier, inc=1, device_id={"slab": partner(b)}, device_id_type=MESH
-        )
-    gw_rows = gw_ref.shape[0]
-    acc[0:gw_rows, :] = gw_ref[...]
-    acc[gw_rows:, :] = gow_ref[...]
-    taps_sum[0] = taps_ref[...]
-    pl.semaphore_wait(barrier, count)
+    for where in [partner(b) for b in bits] + [nxt, prv, mate]:
+        pl.semaphore_signal(barrier, inc=1, device_id=where, device_id_type=MESH)
+    pl.semaphore_wait(barrier, stages + 3)
+
+    down = copy_to(gprev_ref, from_next, h_send.at[0], h_recv.at[0], prv)
+    up = copy_to(gnext_ref, from_prev, h_send.at[1], h_recv.at[1], nxt)
+    mix_copy = copy_to(mix_other_ref, mix_in, m_send, m_recv, mate)
+    down.start()
+    up.start()
+    mix_copy.start()
+    sent = [down, up, mix_copy]
 
     lows = [jnp.int32(0), jnp.int32(span)]
     trail = [[], []]
-    waits = []
-    size = span
-    offset = 0
-    for k in range(count):
-        size //= 2
-        copies = []
-        for t in range(2):
+    step_of = [0, 0]
+    flight = [None, None]
+
+    def rows_at(at, size):
+        return pl.ds(pl.multiple_of(at, 16), size)
+
+    def advance(t):
+        k = step_of[t]
+        if k > 2 * stages:
+            return
+        if flight[t] is not None:
+            flight[t].wait_recv()
+            sent.append(flight[t])
+            if k <= stages:
+                size = span >> k
+                at = rows_at(lows[t], size)
+                offset = span - 2 * size
+                acc[at, :] = acc[at, :] + incoming[t, pl.ds(offset, size), :].astype(F32)
+        if k == stages:
+            at = rows_at(lows[t], span >> stages)
+            final[at, :] = acc[at, :].astype(BF16)
+        if k < stages:
+            size = span >> (k + 1)
             b = orders[t][k]
             bit = bit_of(b)
             keep = lows[t] + bit * size
             give = lows[t] + (1 - bit) * size
-            slots = pl.ds(offset, size)
-            outgoing[t, slots, :] = acc[pl.ds(pl.multiple_of(give, 16), size), :].astype(BF16)
-            copy = pltpu.make_async_remote_copy(
-                src_ref=outgoing.at[t, slots],
-                dst_ref=incoming.at[t, slots],
-                send_sem=s_send.at[t, k],
-                recv_sem=s_recv.at[t, k],
-                device_id={"slab": partner(b)},
-                device_id_type=MESH,
+            slots = pl.ds(span - 2 * size, size)
+            outgoing[t, slots, :] = acc[rows_at(give, size), :].astype(BF16)
+            flight[t] = copy_to(
+                outgoing.at[t, slots],
+                incoming.at[t, slots],
+                s_send.at[t, k],
+                s_recv.at[t, k],
+                partner(b),
+            )
+            flight[t].start()
+            lows[t] = keep
+            trail[t].append(keep)
+        elif k < 2 * stages:
+            j = 2 * stages - 1 - k
+            at = rows_at(trail[t][j], span >> (j + 1))
+            flight[t] = copy_to(
+                final.at[at],
+                final.at[at],
+                s_send.at[t, k],
+                s_recv.at[t, k],
+                partner(orders[t][j]),
+            )
+            flight[t].start()
+        step_of[t] = k + 1
+
+    def weight_gradient(base, g):
+        for index, s_ref in ((tp, so_ref), (1 - tp, st_ref)):
+            product = mm_tn(s_ref[...], g)
+            for half in range(halves):
+                at = pl.multiple_of(base + half * depth + index * width, 128)
+                acc[pl.ds(at, width), :] = product[:, half * 128 : (half + 1) * 128]
+
+    block = depth * halves
+    weight_gradient(0, gq_ref[...])
+    acc[block : 2 * block, :] = gow_ref[...]
+    advance(0)
+    for c in range(chunks):
+        rows = slice(c * CHUNK, (c + 1) * CHUNK)
+        gq = gq_ref[rows, :]
+        own[rows, :] = mm_nt(gq, wq_ref[mine, :])
+        other[rows, :] = mm_nt(gq, wq_ref[theirs, :])
+    advance(0)
+    down.wait_recv()
+    up.wait_recv()
+    parts = []
+    for c in range(chunks):
+        rows = slice(c * CHUNK, (c + 1) * CHUNK)
+        total = gkv_ref[rows, :]
+        if c < edge_chunks:
+            total = total + from_prev[rows, :].astype(F32)
+        if c >= chunks - edge_chunks:
+            edge_rows = slice(c * CHUNK - last, (c + 1) * CHUNK - last)
+            total = total + from_next[edge_rows, :].astype(F32)
+        total = total.astype(BF16)
+        low[rows, :] = total
+        gk, gv = total[:, :cols], total[:, cols:]
+        part_out[rows, :] = (
+            other[rows, :] + mm_nt(gk, wk_ref[theirs, :]) + mm_nt(gv, wv_ref[theirs, :])
+        ).astype(BF16)
+        copy = copy_to(part_out.at[rows], part_in.at[rows], p_send.at[c], p_recv.at[c], mate)
+        copy.start()
+        parts.append(copy)
+        own[rows, :] += mm_nt(gk, wk_ref[mine, :]) + mm_nt(gv, wv_ref[mine, :])
+    advance(0)
+    weight_gradient(2 * block, low[:, :cols])
+    weight_gradient(3 * block, low[:, cols:])
+    advance(1)
+    advance(0)
+    advance(1)
+    mix_copy.wait_recv()
+    layer_ref[...] = (
+        so_ref[...].astype(F32) + (mix_ref[...] + mix_in[...].astype(F32))
+    ).astype(BF16)
+    advance(0)
+    edges_low, edges_high = [], []
+    for c in range(chunks):
+        rows = slice(c * CHUNK, (c + 1) * CHUNK)
+        parts[c].wait_recv()
+        stem_grad = cot_ref[rows, :].astype(F32) + (own[rows, :] + part_in[rows, :].astype(F32))
+        own[rows, :] = stem_grad
+        edge[rows, :] = stem_grad.astype(BF16)
+        if c < edge_chunks:
+            copy = copy_to(
+                edge.at[rows], edge_next.at[rows], e_send.at[0, c], e_recv.at[0, c], prv
             )
             copy.start()
-            copies.append(copy)
-            lows[t] = keep
-            trail[t].append(keep)
-        b = orders[0][k]
-        taps_copy = pltpu.make_async_remote_copy(
-            src_ref=taps_sum.at[k],
-            dst_ref=taps_in.at[k],
-            send_sem=t_send.at[k],
-            recv_sem=t_recv.at[k],
-            device_id={"slab": partner(b)},
-            device_id_type=MESH,
-        )
-        taps_copy.start()
-        for t in range(2):
-            copies[t].wait_recv()
-            at = pl.ds(pl.multiple_of(lows[t], 16), size)
-            acc[at, :] = acc[at, :] + incoming[t, pl.ds(offset, size), :].astype(F32)
-        taps_copy.wait_recv()
-        taps_sum[k + 1] = taps_sum[k] + taps_in[k]
-        waits += copies + [taps_copy]
-        offset += size
-    for t in range(2):
-        at = pl.ds(pl.multiple_of(lows[t], 16), size)
-        final[at, :] = acc[at, :].astype(BF16)
-    for k in range(count - 1, -1, -1):
-        copies = []
-        for t in range(2):
-            at = pl.ds(pl.multiple_of(trail[t][k], 16), size)
-            copy = pltpu.make_async_remote_copy(
-                src_ref=final.at[at],
-                dst_ref=final.at[at],
-                send_sem=g_send.at[t, k],
-                recv_sem=g_recv.at[t, k],
-                device_id={"slab": partner(orders[t][k])},
-                device_id_type=MESH,
+            edges_low.append(copy)
+        if c >= chunks - edge_chunks:
+            e = c - (chunks - edge_chunks)
+            edge_rows = slice(e * CHUNK, (e + 1) * CHUNK)
+            copy = copy_to(
+                edge.at[rows], edge_prev.at[edge_rows], e_send.at[1, e], e_recv.at[1, e], nxt
             )
             copy.start()
-            copies.append(copy)
-        for copy in copies:
+            edges_high.append(copy)
+        if c % 2 == 0:
+            advance(1)
+    advance(0)
+    sums = [jnp.zeros((1, width), F32) for _ in range(3)]
+    for c in range(chunks):
+        rows = slice(c * CHUNK, (c + 1) * CHUNK)
+        g = own[rows, :]
+        if c < edge_chunks:
+            before = tok_prev_ref[rows, :]
+        else:
+            before = tok_ref[(c - edge_chunks) * CHUNK : (c - edge_chunks + 1) * CHUNK, :]
+        if c >= chunks - edge_chunks:
+            e = c - (chunks - edge_chunks)
+            after = tok_next_ref[e * CHUNK : (e + 1) * CHUNK, :]
+        else:
+            after = tok_ref[(c + edge_chunks) * CHUNK : (c + edge_chunks + 1) * CHUNK, :]
+        for n, x in enumerate((before, tok_ref[rows, :], after)):
+            sums[n] = sums[n] + jnp.sum(g * x.astype(F32), axis=0, keepdims=True)
+    taps_sum[0] = jnp.concatenate(sums + [jnp.zeros((5, width), F32)], axis=0)
+
+    def send_taps(k):
+        copy = copy_to(
+            taps_sum.at[k], taps_in.at[k], t_send.at[k], t_recv.at[k], partner(bits[k])
+        )
+        copy.start()
+        return copy
+
+    def take_taps(k, copy):
+        copy.wait_recv()
+        sent.append(copy)
+        taps_sum[k + 1] = taps_sum[k] + taps_in[k]
+
+    def finish_tokens():
+        for copy in edges_low + edges_high:
             copy.wait_recv()
-        waits += copies
-        size *= 2
-    for copy in waits:
+        for c in range(chunks):
+            rows = slice(c * CHUNK, (c + 1) * CHUNK)
+            if c < edge_chunks:
+                before = edge_prev[rows, :].astype(F32)
+            else:
+                before = own[(c - edge_chunks) * CHUNK : (c - edge_chunks + 1) * CHUNK, :]
+            if c >= chunks - edge_chunks:
+                e = c - (chunks - edge_chunks)
+                after = edge_next[e * CHUNK : (e + 1) * CHUNK, :].astype(F32)
+            else:
+                after = own[(c + edge_chunks) * CHUNK : (c + edge_chunks + 1) * CHUNK, :]
+            grad_ref[rows, :] = (
+                taps_ref[0:1, :] * after + taps_ref[1:2, :] * own[rows, :]
+                + taps_ref[2:3, :] * before
+            )
+
+    for k in range(stages):
+        copy = send_taps(k)
+        advance(1)
+        advance(0)
+        if k == 1:
+            finish_tokens()
+        take_taps(k, copy)
+    if stages < 2:
+        finish_tokens()
+    for _ in range(2 * stages):
+        advance(0)
+        advance(1)
+    taps_out_ref[...] = taps_sum[stages]
+    for copy in sent + parts + edges_low + edges_high:
         copy.wait_send()
-    depth, cols = gqw_ref.shape
+
+
+def unpack_kernel(final_ref, taps_in_ref, gqw_ref, gkw_ref, gvw_ref, go_ref, taps_ref):
     at = 0
-    for out in (gqw_ref, gkw_ref, gvw_ref, go_ref):
+    for out in (gqw_ref, go_ref, gkw_ref, gvw_ref):
         rows = out.shape[0]
         for half in range(out.shape[1] // 128):
-            out[:, half * 128 : (half + 1) * 128] = final[at : at + rows, :].astype(F32)
+            out[:, half * 128 : (half + 1) * 128] = final_ref[at : at + rows, :].astype(F32)
             at += rows
-    taps_out_ref[...] = taps_sum[count]
-
-
-def reduce_all(gw, gow, taps, depth, cols, slabs):
-    rows = gw.shape[0] + gow.shape[0]
-    bits = tuple(range(slabs.bit_length() - 1))
-    count = len(bits)
-    shapes = [jax.ShapeDtypeStruct((depth, cols), F32)] * 3
-    shapes.append(jax.ShapeDtypeStruct((cols, depth), F32))
-    shapes.append(jax.ShapeDtypeStruct(taps.shape, F32))
-    dma = pltpu.SemaphoreType.DMA
-    return pl.pallas_call(
-        functools.partial(reduce_kernel, bits),
-        out_shape=shapes,
-        in_specs=[VMEM] * 3,
-        out_specs=[VMEM] * 5,
-        scratch_shapes=[
-            pltpu.VMEM((rows, 128), F32),
-            pltpu.VMEM((2, rows // 2, 128), BF16),
-            pltpu.VMEM((2, rows // 2, 128), BF16),
-            pltpu.VMEM((rows, 128), BF16),
-            pltpu.VMEM((count,) + taps.shape, F32),
-            pltpu.VMEM((count + 1,) + taps.shape, F32),
-            dma((2, count)),
-            dma((2, count)),
-            dma((2, count)),
-            dma((2, count)),
-            dma((count,)),
-            dma((count,)),
-        ],
-        compiler_params=pltpu.CompilerParams(
-            collective_id=0, has_side_effects=True, vmem_limit_bytes=LIMIT
-        ),
-    )(gw, gow, taps)
+    taps_ref[...] = taps_in_ref[0:3, :]
 
 
 def body(
@@ -418,8 +507,10 @@
     def swap(x):
         return lax.ppermute(x, "tp", [(0, 1), (1, 0)])
 
-    before = jnp.concatenate([to_next(tokens[count - plane :]), tokens[: count - plane]])
-    after = jnp.concatenate([tokens[plane:], to_prev(tokens[:plane])])
+    tok_prev = to_next(tokens[count - plane :])
+    tok_next = to_prev(tokens[:plane])
+    before = jnp.concatenate([tok_prev, tokens[: count - plane]])
+    after = jnp.concatenate([tokens[plane:], tok_next])
     before_f, own_f, after_f = before.astype(F32), tokens.astype(F32), after.astype(F32)
     stem = (stem_taps[0] * before_f + stem_taps[1] * own_f + stem_taps[2] * after_f).astype(BF16)
     stem_other = swap(stem)
@@ -457,34 +548,81 @@
         ],
         compiler_params=params,
     )(key_blocks, counts, q, kv, kv_prev, kv_next, cotangent, cot_other, out_weight)
-    from_next = to_prev(gprev)
-    from_prev = to_next(gnext)
-    layer_out = (stem.astype(F32) + (mix + swap(mix_other).astype(F32))).astype(BF16)
-
-    own, other, gw = pl.pallas_call(
-        gradient_kernel,
+    stages = slabs.bit_length() - 1
+    chunks = count // CHUNK
+    edge_chunks = plane // CHUNK
+    rows = 4 * depth * cols // 128
+    dma = pltpu.SemaphoreType.DMA
+    layer_out, grad_tokens, final, taps = pl.pallas_call(
+        functools.partial(backward_kernel, slabs),
         out_shape=[
+            sds((count, width), BF16),
             sds((count, width), F32),
-            sds((count, width), BF16),
-            sds((3 * depth * cols // 128, 128), F32),
+            sds((rows, 128), BF16),
+            sds((8, width), F32),
         ],
-        in_specs=[VMEM] * 9,
-        out_specs=[VMEM] * 3,
-        scratch_shapes=[pltpu.VMEM((count, 2 * cols), BF16)],
+        in_specs=[VMEM] * 17,
+        out_specs=[VMEM] * 4,
+        scratch_shapes=[
+            pltpu.VMEM((count, 2 * cols), BF16),
+            pltpu.VMEM((plane, 2 * cols), BF16),
+            pltpu.VMEM((plane, 2 * cols), BF16),
+            pltpu.VMEM((count, width), BF16),
+            pltpu.VMEM((count, width), F32),
+            pltpu.VMEM((count, width), F32),
+            pltpu.VMEM((count, width), BF16),
+            pltpu.VMEM((count, width), BF16),
+            pltpu.VMEM((count, width), BF16),
+            pltpu.VMEM((plane, width), BF16),
+            pltpu.VMEM((plane, width), BF16),
+            pltpu.VMEM((rows, 128), F32),
+            pltpu.VMEM((2, rows // 2, 128), BF16),
+            pltpu.VMEM((2, rows // 2, 128), BF16),
+            pltpu.VMEM((stages, 8, width), F32),
+            pltpu.VMEM((stages + 1, 8, width), F32),
+            dma((2,)),
+            dma((2,)),
+            dma,
+            dma,
+            dma((chunks,)),
+            dma((chunks,)),
+            dma((2, edge_chunks)),
+            dma((2, edge_chunks)),
+            dma((2, 2 * stages)),
+            dma((2, 2 * stages)),
+            dma((stages,)),
+            dma((stages,)),
+        ],
+        compiler_params=pltpu.CompilerParams(
+            collective_id=1, has_side_effects=True, vmem_limit_bytes=LIMIT
+        ),
+    )(
+        gq,
+        gkv,
+        gprev,
+        gnext,
+        stem,
+        stem_other,
+        query_weight,
+        key_weight,
+        value_weight,
+        gow,
+        mix,
+        mix_other,
+        cotangent,
+        tokens,
+        tok_prev,
+        tok_next,
+        stem_taps,
+    )
+    gqw, gkw, gvw, go, grad_taps = pl.pallas_call(
+        unpack_kernel,
+        out_shape=[sds((depth, cols), F32)] * 3
+        + [sds((cols, depth), F32), sds(stem_taps.shape, F32)],
+        in_specs=[VMEM] * 2,
+        out_specs=[VMEM] * 5,
         compiler_params=params,
-    )(gq, gkv, from_prev, from_next, stem, stem_other, query_weight, key_weight, value_weight)
-
-    grad_stem = cotangent.astype(F32) + (own + swap(other).astype(F32))
-    grad_low = grad_stem.astype(BF16)
-    grad_prev = to_next(grad_low[count - plane :]).astype(F32)
-    grad_next = to_prev(grad_low[:plane]).astype(F32)
-    grad_after = jnp.concatenate([grad_stem[plane:], grad_next])
-    grad_before = jnp.concatenate([grad_prev, grad_stem[: count - plane]])
-    grad_tokens = (
-        stem_taps[0] * grad_after + stem_taps[1] * grad_stem + stem_taps[2] * grad_before
-    )
-    taps = jnp.stack([jnp.sum(grad_stem * x, axis=0) for x in (before_f, own_f, after_f)])
-    gqw, gkw, gvw, go, grad_taps = reduce_all(gw, gow, taps, depth, cols, slabs)
+    )(final, taps)
     return (layer_out, grad_tokens, grad_taps, gqw, gkw, gvw, go)
 
 

time: 154 us -> 130 us (0.84)
  waiting for transfers between devices: 45.2 us -> 25.7 us
  Pallas kernels: 66 us -> 80.4 us
  starting transfers between devices: 25.1 us -> 12.4 us
  other arithmetic: 4.74 us -> 1.52 us
  local copies, waits for them, and re-layouts: 11.3 us -> 9.11 us
    pallas_call x2, Pallas kernels: 42.6 us -> 57.2 us  [the longest x1 54.5 us: body(): pl.pallas_call(functools.partial(backward_kernel, slabs), out_shape=[sds(...]
    ppermute x4 -> x2, waiting for transfers between devices: 21.5 us -> 11.7 us  [swap(): return lax.ppermute(x, 'tp', [(0, 1), (1, 0)])]
    ppermute x4 -> x2, waiting for transfers between devices: 17.4 us -> 7.68 us  [to_next(): return lax.ppermute(x, 'slab', up)]
    ppermute x4 -> x2, starting transfers between devices: 17.9 us -> 9.67 us  [to_prev(): return lax.ppermute(x, 'slab', down)]
    ppermute x4 -> x2, starting transfers between devices: 5.7 us -> 2.14 us  [swap(): return lax.ppermute(x, 'tp', [(0, 1), (1, 0)])]
    unnamed x44 -> x23, local copies, waits for them, and re-layouts: 7.04 us -> 5.13 us
    ppermute x4 -> x2, waiting for transfers between devices: 6.34 us -> 6.33 us  [to_prev(): return lax.ppermute(x, 'slab', down)]
  transfers between devices with their start and end apart: 12 -> 6, of which waited for: 7 -> 4; matrix products, arithmetic and copies ran while one was open for 3% -> 3% of each run, Pallas kernels for 7% -> 3%
where the time goes in v2:
time: 130 us
  Pallas kernels  80.4 us (62%)
  waiting for transfers between devices  25.7 us (20%)
  starting transfers between devices  12.4 us (10%)
  local copies, waits for them, and re-layouts  9.11 us (7%)
  other arithmetic  1.52 us (1%)
    pallas_call x1, Pallas kernels, body(): pl.pallas_call(functools.partial(backward_kernel, slabs), out_shape=[sds(...  54.5 us
    pallas_call x1, Pallas kernels, body(): pl.pallas_call(functools.partial(attention_kernel, slabs), out_shape=[sds...  19.2 us
    ppermute x2, waiting for transfers between devices, swap(): return lax.ppermute(x, 'tp', [(0, 1), (1, 0)])  11.7 us
    ppermute x2, starting transfers between devices, to_prev(): return lax.ppermute(x, 'slab', down)  9.67 us
    ppermute x2, waiting for transfers between devices, to_next(): return lax.ppermute(x, 'slab', up)  7.68 us
    ppermute x2, waiting for transfers between devices, to_prev(): return lax.ppermute(x, 'slab', down)  6.33 us
    unnamed x23, local copies, waits for them, and re-layouts  5.13 us
    pallas_call x1, Pallas kernels, body(): pl.pallas_call(project_kernel, out_shape=[sds((count, cols), BF16), sds((...  3.92 us
  transfers between devices with their start and end apart: 6, of which 4 were waited for; matrix products, arithmetic and copies ran while one was open for 3% of the time, Pallas kernels for 3%

profile of v2, /device:TPU:0, one launch (start us, length us, event | category | flops | bytes accessed | tf_op | source)
XLA Modules:
  0.0 129.8 jit_solution(3124981100511086772)
XLA Ops:
  0.6 0.0 copy-start.1
  0.6 1.1 fusion.1
  1.8 0.5 collective-permute-start
  2.3 5.0 %collective-permute-start.1 = (bf16[512,256]{1,0:T(8,128)(2,1)S(1)}, bf16[512,256]{1,0:T(8,128)(2,1)S(1)}, u32[]{:S(2)}, u32[]{:S(2)}) collective-permute-start(bf16[512,256]{1,0:T(8,128)(2,1)S(1)} %get-tuple-element.46), channel_id=1, source_target_pairs={{0,30},{2,0},{4,2},{6,4},{8,6},{10,8},{12,10},{14,12},{16,14},{18,... | collective-permute-start | bytes 786440 | tf_op jit(solution)/shard_map/ppermute | solution.py:505
  7.3 0.8 fusion.2
  8.1 3.3 %collective-permute-done.tok_prev_ref = bf16[512,256]{1,0:T(8,128)(2,1)S(1)} collective-permute-done((bf16[512,256]{1,0:T(8,128)(2,1)S(1)}, bf16[512,256]{1,0:T(8,128)(2,1)S(1)}, u32[]{:S(2)}, u32[]{:S(2)}) %collective-permute-start) | collective-permute-done | bytes 262176 | tf_op jit(solution)/shard_map/ppermute | solution.py:502
  11.4 0.0 collective-permute-done.1.tok_next_ref
  11.4 1.5 %add_convert_fusion.so_ref = bf16[1024,256]{1,0:T(8,128)(2,1)S(1)} fusion(bf16[1024,256]{1,0:T(8,128)(2,1)} %tok_ref.1, bf16[512,256]{1,0:T(8,128)(2,1)S(1)} %get-tuple-element.46, bf16[512,256]{1,0:T(8,128)(2,1)S(1)} %collective-permute-done.tok_prev_ref, bf16[512,256]{1,0:T(8,128)(2,1)S(1)} %collective-permute-done.1.tok_next_ref, ...), kind=kLoop, calls=%fused_computation | loop fusion | flops 3932160 | bytes 2100224 | tf_op jit(solution)/shard_map/convert_element_type | solution.py:515
  13.0 0.0 copy-start
  13.0 0.0 copy-start.9
  13.0 2.1 %collective-permute-start.2 = (bf16[1024,256]{1,0:T(8,128)(2,1)S(1)}, bf16[1024,256]{1,0:T(8,128)(2,1)S(1)}, u32[]{:S(2)}, u32[]{:S(2)}) collective-permute-start(bf16[1024,256]{1,0:T(8,128)(2,1)S(1)} %add_convert_fusion.so_ref), channel_id=1, source_target_pairs={{0,1},{1,0},{2,3},{3,2},{4,5},{5,4},{6,7},{7,6},{8,9},{9,8},{10,11... | collective-permute-start | bytes 1572872 | tf_op jit(solution)/shard_map/ppermute | solution.py:508
  15.0 0.0 copy-done.1
  15.0 0.1 collective-permute-start.5
  15.1 11.7 %collective-permute-done.2.st_ref = bf16[1024,256]{1,0:T(8,128)(2,1)S(1)} collective-permute-done((bf16[1024,256]{1,0:T(8,128)(2,1)S(1)}, bf16[1024,256]{1,0:T(8,128)(2,1)S(1)}, u32[]{:S(2)}, u32[]{:S(2)}) %collective-permute-start.2) | collective-permute-done | bytes 524320 | tf_op jit(solution)/shard_map/ppermute | solution.py:508
  26.8 0.8 copy-done.2
  27.6 3.9 %shard_map.144 = (bf16[1024,256]{1,0:T(8,128)(2,1)}, bf16[1024,512]{1,0:T(8,128)(2,1)}) custom-call(bf16[1024,256]{1,0:T(8,128)(2,1)} %copy-done, bf16[1024,256]{1,0:T(8,128)(2,1)} %copy-done.2, bf16[512,256]{1,0:T(8,128)(2,1)} %wq_ref.3, bf16[512,256]{1,0:T(8,128)(2,1)} %wk_ref.3, bf16[512,256]{1,0:T(8,128)(2,1)} %wv_ref.3), custom_call_target="tpu_custom_call" | custom-call | tf_op jit(solution)/shard_map/pallas_call | solution.py:519
  31.5 2.1 %fusion = (bf16[512,512]{1,0:T(8,128)(2,1)}, bf16[512,512]{1,0:T(8,128)(2,1)S(1)}) fusion(bf16[1024,512]{1,0:T(8,128)(2,1)} %get-tuple-element.26.kv_ref), kind=kLoop, calls=%fused_computation.1 | loop fusion | bytes 2097152 | tf_op jit(solution)/shard_map/slice | solution.py:527
  33.6 0.0 copy-done.4
  33.6 4.7 %collective-permute-start.4 = (bf16[512,512]{1,0:T(8,128)(2,1)}, bf16[512,512]{1,0:T(8,128)(2,1)S(1)}, u32[]{:S(2)}, u32[]{:S(2)}) collective-permute-start(bf16[512,512]{1,0:T(8,128)(2,1)} %get-tuple-element.43), channel_id=1, source_target_pairs={{0,30},{2,0},{4,2},{6,4},{8,6},{10,8},{12,10},{14,12},{16,14},{18,... | collective-permute-start | bytes 1572872 | tf_op jit(solution)/shard_map/ppermute | solution.py:505
  38.3 0.0 collective-permute-start.3
  38.3 0.7 copy.16.blocks_ref
  38.9 0.0 collective-permute-done.5.ct_ref
  38.9 6.3 %collective-permute-done.4.kv_next_ref = bf16[512,512]{1,0:T(8,128)(2,1)S(1)} collective-permute-done((bf16[512,512]{1,0:T(8,128)(2,1)}, bf16[512,512]{1,0:T(8,128)(2,1)S(1)}, u32[]{:S(2)}, u32[]{:S(2)}) %collective-permute-start.4) | collective-permute-done | bytes 524320 | tf_op jit(solution)/shard_map/ppermute | solution.py:505
  45.3 4.4 %collective-permute-done.3.kv_prev_ref = bf16[512,512]{1,0:T(8,128)(2,1)S(1)} collective-permute-done((bf16[512,512]{1,0:T(8,128)(2,1)S(1)}, bf16[512,512]{1,0:T(8,128)(2,1)S(1)}, u32[]{:S(2)}, u32[]{:S(2)}) %collective-permute-start.3) | collective-permute-done | bytes 524320 | tf_op jit(solution)/shard_map/ppermute | solution.py:502
  49.7 0.8 copy-done.8
  50.5 19.2 %shard_map.145 = (bf16[1024,256]{1,0:T(8,128)(2,1)}, f32[1024,512]{1,0:T(8,128)}, bf16[512,512]{1,0:T(8,128)(2,1)}, bf16[512,512]{1,0:T(8,128)(2,1)}, f32[1024,2...) custom-call(s32[8,4]{1,0:T(8,128)} %copy.16.blocks_ref, s32[8]{0:T(128)} %counts_ref.1, ...), custom_call_target="tpu_custom_call" | custom-call | tf_op jit(solution)/shard_map/pallas_call | solution.py:529
  69.7 54.5 %shard_map.146 = (bf16[1024,256]{1,0:T(8,128)(2,1)}, f32[1024,256]{1,0:T(8,128)}, bf16[4096,128]{1,0:T(8,128)(2,1)}, f32[8,256]{1,0:T(8,128)}) custom-call(bf16[1024,256]{1,0:T(8,128)(2,1)} %get-tuple-element.27.gq_ref, f32[1024,512]{1,0:T(8,128)} %get-tuple-element.28.gkv_ref, bf16[512,512]{1,0:T(8,128)(2,1)} %get-tuple-element.29.gprev_ref, ...), custom_call_target="tpu_custom_call" | custom-call | tf_op jit(solution)/shard_map/pallas_call | solution.py:556
  124.2 0.0 copy-start.5
  124.3 2.7 %shard_map.147 = (f32[512,256]{1,0:T(8,128)}, f32[512,256]{1,0:T(8,128)}, f32[512,256]{1,0:T(8,128)}, f32[256,512]{1,0:T(8,128)}, f32[3,256]{1,0:T(4,128)}) custom-call(bf16[4096,128]{1,0:T(8,128)(2,1)} %get-tuple-element.36.final_ref, f32[8,256]{1,0:T(8,128)} %get-tuple-element.37.taps_in_ref), custom_call_target="tpu_custom_call" | custom-call | tf_op jit(solution)/shard_map/pallas_call | solution.py:618
  126.9 1.9 %copy.19 = bf16[1024,256]{1,0:T(8,128)(2,1)} copy(bf16[1024,256]{1,0:T(8,128)(2,1)} %get-tuple-element.57) | data formatting | bytes 1048576
  128.8 0.0 copy-done.5
  128.8 1.0 copy.20
  (11 shorter events, 0.0 us)
Async XLA Ops:
  0.6 14.4 %copy-start.1 = (bf16[1024,256]{1,0:T(8,128)(2,1)S(1)}, bf16[1024,256]{1,0:T(8,128)(2,1)}, u32[]{:S(2)}) copy-start(bf16[1024,256]{1,0:T(8,128)(2,1)} %cot_ref.1) | copy-start | bytes 1572868
  1.8 9.7 %collective-permute-start = (bf16[512,256]{1,0:T(8,128)(2,1)S(1)}, bf16[512,256]{1,0:T(8,128)(2,1)S(1)}, u32[]{:S(2)}, u32[]{:S(2)}) collective-permute-start(bf16[512,256]{1,0:T(8,128)(2,1)S(1)} %get-tuple-element.45), channel_id=1, source_target_pairs={{0,2},{2,4},{4,6},{6,8},{8,10},{10,12},{12,14},{14,16},{16,18},{18... | collective-permute-start | bytes 786440 | tf_op jit(solution)/shard_map/ppermute | solution.py:502
  2.3 9.1 %collective-permute-start.1 = (bf16[512,256]{1,0:T(8,128)(2,1)S(1)}, bf16[512,256]{1,0:T(8,128)(2,1)S(1)}, u32[]{:S(2)}, u32[]{:S(2)}) collective-permute-start(bf16[512,256]{1,0:T(8,128)(2,1)S(1)} %get-tuple-element.46), channel_id=1, source_target_pairs={{0,30},{2,0},{4,2},{6,4},{8,6},{10,8},{12,10},{14,12},{16,14},{18,... | collective-permute-start | bytes 786440 | tf_op jit(solution)/shard_map/ppermute | solution.py:505
  11.4 22.2 %copy-start.3 = (bf16[512,256]{1,0:T(8,128)(2,1)}, bf16[512,256]{1,0:T(8,128)(2,1)S(1)}, u32[]{:S(2)}) copy-start(bf16[512,256]{1,0:T(8,128)(2,1)S(1)} %collective-permute-done.tok_prev_ref) | copy-start | bytes 786436
  11.4 22.2 %copy-start.4 = (bf16[512,256]{1,0:T(8,128)(2,1)}, bf16[512,256]{1,0:T(8,128)(2,1)S(1)}, u32[]{:S(2)}) copy-start(bf16[512,256]{1,0:T(8,128)(2,1)S(1)} %collective-permute-done.1.tok_next_ref) | copy-start | bytes 786436
  13.0 13.9 %copy-start = (bf16[1024,256]{1,0:T(8,128)(2,1)}, bf16[1024,256]{1,0:T(8,128)(2,1)S(1)}, u32[]{:S(2)}) copy-start(bf16[1024,256]{1,0:T(8,128)(2,1)S(1)} %add_convert_fusion.so_ref) | copy-start | bytes 1572868
  13.0 25.3 %copy-start.9 = (s32[8,4]{0,1:T(4,128)S(1)}, s32[8,4]{0,1:T(4,128)}, u32[]{:S(2)}) copy-start(s32[8,4]{0,1:T(4,128)} %param.15) | copy-start | bytes 388
  13.0 13.8 %collective-permute-start.2 = (bf16[1024,256]{1,0:T(8,128)(2,1)S(1)}, bf16[1024,256]{1,0:T(8,128)(2,1)S(1)}, u32[]{:S(2)}, u32[]{:S(2)}) collective-permute-start(bf16[1024,256]{1,0:T(8,128)(2,1)S(1)} %add_convert_fusion.so_ref), channel_id=1, source_target_pairs={{0,1},{1,0},{2,3},{3,2},{4,5},{5,4},{6,7},{7,6},{8,9},{9,8},{10,11... | collective-permute-start | bytes 1572872 | tf_op jit(solution)/shard_map/ppermute | solution.py:508
  15.0 23.9 %collective-permute-start.5 = (bf16[1024,256]{1,0:T(8,128)(2,1)S(1)}, bf16[1024,256]{1,0:T(8,128)(2,1)S(1)}, u32[]{:S(2)}, u32[]{:S(2)}) collective-permute-start(bf16[1024,256]{1,0:T(8,128)(2,1)S(1)} %copy-done.1), channel_id=1, source_target_pairs={{0,1},{1,0},{2,3},{3,2},{4,5},{5,4},{6,7},{7,6},{8,9},{9,8},{10,11... | collective-permute-start | bytes 1572872 | tf_op jit(solution)/shard_map/ppermute | solution.py:508
  26.8 0.8 copy-start.2
  33.6 11.7 %collective-permute-start.4 = (bf16[512,512]{1,0:T(8,128)(2,1)}, bf16[512,512]{1,0:T(8,128)(2,1)S(1)}, u32[]{:S(2)}, u32[]{:S(2)}) collective-permute-start(bf16[512,512]{1,0:T(8,128)(2,1)} %get-tuple-element.43), channel_id=1, source_target_pairs={{0,30},{2,0},{4,2},{6,4},{8,6},{10,8},{12,10},{14,12},{16,14},{18,... | collective-permute-start | bytes 1572872 | tf_op jit(solution)/shard_map/ppermute | solution.py:505
  38.3 11.4 %collective-permute-start.3 = (bf16[512,512]{1,0:T(8,128)(2,1)S(1)}, bf16[512,512]{1,0:T(8,128)(2,1)S(1)}, u32[]{:S(2)}, u32[]{:S(2)}) collective-permute-start(bf16[512,512]{1,0:T(8,128)(2,1)S(1)} %get-tuple-element.44), channel_id=1, source_target_pairs={{0,2},{2,4},{4,6},{6,8},{8,10},{10,12},{12,14},{14,16},{16,18},{18... | collective-permute-start | bytes 1572872 | tf_op jit(solution)/shard_map/ppermute | solution.py:502
  38.9 10.7 %copy-start.6 = (bf16[1024,256]{1,0:T(8,128)(2,1)}, bf16[1024,256]{1,0:T(8,128)(2,1)S(1)}, u32[]{:S(2)}) copy-start(bf16[1024,256]{1,0:T(8,128)(2,1)S(1)} %collective-permute-done.5.ct_ref) | copy-start | bytes 1572868
  45.3 4.4 %copy-start.7 = (bf16[512,512]{1,0:T(8,128)(2,1)}, bf16[512,512]{1,0:T(8,128)(2,1)S(1)}, u32[]{:S(2)}) copy-start(bf16[512,512]{1,0:T(8,128)(2,1)S(1)} %collective-permute-done.4.kv_next_ref) | copy-start | bytes 1572868
  49.7 0.8 copy-start.8
  124.2 4.6 %copy-start.5 = (f32[1024,256]{1,0:T(8,128)S(1)}, f32[1024,256]{1,0:T(8,128)}, u32[]{:S(2)}) copy-start(f32[1024,256]{1,0:T(8,128)} %get-tuple-element.58) | copy-start | bytes 3145732

commit v3 on v2

--- a/solution.py
+++ b/solution.py
@@ -17,7 +17,6 @@
 MESH = pl.DeviceIdType.MESH
 VMEM = pl.BlockSpec(memory_space=pltpu.VMEM)
 SMEM = pl.BlockSpec(memory_space=pltpu.SMEM)
-ANY = pl.BlockSpec(memory_space=pl.ANY)
 LIMIT = 60 * 1024 * 1024
 CHUNK = 256
 
@@ -38,23 +37,154 @@
     return pl.ds(pl.multiple_of(index * width, width), width)
 
 
-def project_kernel(so_ref, st_ref, wq_ref, wk_ref, wv_ref, q_ref, kv_ref):
+def copy_to(src, dst, send, recv, where):
+    return pltpu.make_async_remote_copy(
+        src_ref=src,
+        dst_ref=dst,
+        send_sem=send,
+        recv_sem=recv,
+        device_id=where,
+        device_id_type=MESH,
+    )
+
+
+def forward_kernel(
+    slabs,
+    tok_ref,
+    taps_ref,
+    wq_ref,
+    wk_ref,
+    wv_ref,
+    ow_ref,
+    cot_ref,
+    so_ref,
+    st_ref,
+    ct_ref,
+    prev_ref,
+    next_ref,
+    q_ref,
+    ext_ref,
+    grad_ref,
+    t_send,
+    t_recv,
+    s_send,
+    s_recv,
+    c_send,
+    c_recv,
+    k_send,
+    k_recv,
+):
+    me = lax.axis_index("slab")
     tp = lax.axis_index("tp")
-    width = so_ref.shape[1]
+    tokens, width = tok_ref.shape
     cols = wq_ref.shape[1]
-    mine, other = part(tp, width), part(1 - tp, width)
-
-    @pl.loop(0, so_ref.shape[0] // CHUNK)
-    def _(step):
-        rows = part(step, CHUNK)
+    chunks = tokens // CHUNK
+    edge_chunks = PLANE_TOK // CHUNK
+    last = tokens - PLANE_TOK
+    mine, theirs = part(tp, width), part(1 - tp, width)
+    nxt = {"slab": lax.rem(me + 1, slabs)}
+    prv = {"slab": lax.rem(me + slabs - 1, slabs)}
+    mate = {"tp": 1 - tp}
+    barrier = pltpu.get_barrier_semaphore()
+    for where in (nxt, prv, mate):
+        pl.semaphore_signal(barrier, inc=1, device_id=where, device_id_type=MESH)
+    pl.semaphore_wait(barrier, 3)
+
+    def rows_of(c):
+        return slice(c * CHUNK, (c + 1) * CHUNK)
+
+    halo = [[], []]
+    for e in range(edge_chunks):
+        rows = rows_of(e)
+        high = slice(last + e * CHUNK, last + (e + 1) * CHUNK)
+        up = copy_to(tok_ref.at[high], prev_ref.at[rows], t_send.at[0, e], t_recv.at[0, e], nxt)
+        down = copy_to(tok_ref.at[rows], next_ref.at[rows], t_send.at[1, e], t_recv.at[1, e], prv)
+        up.start()
+        down.start()
+        halo[0].append(up)
+        halo[1].append(down)
+    order = sorted(range(chunks), key=lambda c: (c % edge_chunks, c))
+    cots = [
+        copy_to(cot_ref.at[rows_of(c)], ct_ref.at[rows_of(c)], c_send.at[c], c_recv.at[c], mate)
+        for c in range(chunks)
+    ]
+    early = chunks // 2
+    for c in range(early):
+        cots[c].start()
+    stems = {}
+    for c in order:
+        rows = rows_of(c)
+        if c < edge_chunks:
+            halo[0][c].wait_recv()
+            before = prev_ref[rows, :]
+        else:
+            before = tok_ref[rows_of(c - edge_chunks), :]
+        if c >= chunks - edge_chunks:
+            e = c - (chunks - edge_chunks)
+            halo[1][e].wait_recv()
+            after = next_ref[rows_of(e), :]
+        else:
+            after = tok_ref[rows_of(c + edge_chunks), :]
+        so_ref[rows, :] = (
+            taps_ref[0:1, :] * before.astype(F32)
+            + taps_ref[1:2, :] * tok_ref[rows, :].astype(F32)
+            + taps_ref[2:3, :] * after.astype(F32)
+        ).astype(BF16)
+        stems[c] = copy_to(so_ref.at[rows], st_ref.at[rows], s_send.at[c], s_recv.at[c], mate)
+        stems[c].start()
+    for c in range(early, chunks):
+        cots[c].start()
+
+    def output_gradient(c):
+        rows = rows_of(c)
+        cots[c].wait_recv()
+        grad_ref[rows, :] = (
+            mm_nt(cot_ref[rows, :], ow_ref[:, mine]) + mm_nt(ct_ref[rows, :], ow_ref[:, theirs])
+        ).astype(BF16)
+
+    for c in range(early):
+        output_gradient(c)
+    edges = []
+    for c in order:
+        rows = rows_of(c)
+        stems[c].wait_recv()
         so, st = so_ref[rows, :], st_ref[rows, :]
 
         def project(w_ref):
-            return (mm(so, w_ref[mine, :]) + mm(st, w_ref[other, :])).astype(BF16)
-
+            return (mm(so, w_ref[mine, :]) + mm(st, w_ref[theirs, :])).astype(BF16)
+
+        place = slice(PLANE_TOK + c * CHUNK, PLANE_TOK + (c + 1) * CHUNK)
+        ext_ref[place, 0:cols] = project(wk_ref)
+        ext_ref[place, cols : 2 * cols] = project(wv_ref)
+        if c < edge_chunks:
+            at = PLANE_TOK + tokens + c * CHUNK
+            copy = copy_to(
+                ext_ref.at[place],
+                ext_ref.at[at : at + CHUNK],
+                k_send.at[0, c],
+                k_recv.at[0, c],
+                prv,
+            )
+            copy.start()
+            edges.append(copy)
+        if c >= chunks - edge_chunks:
+            e = c - (chunks - edge_chunks)
+            copy = copy_to(
+                ext_ref.at[place],
+                ext_ref.at[rows_of(e)],
+                k_send.at[1, e],
+                k_recv.at[1, e],
+                nxt,
+            )
+            copy.start()
+            edges.append(copy)
         q_ref[rows, :] = project(wq_ref)
-        kv_ref[rows, 0:cols] = project(wk_ref)
-        kv_ref[rows, cols : 2 * cols] = project(wv_ref)
+    for c in range(early, chunks):
+        output_gradient(c)
+    for copy in edges:
+        copy.wait_recv()
+    for copy in halo[0] + halo[1] + cots + list(stems.values()) + edges:
+        copy.wait_send()
 
 
 def attention_kernel(
@@ -62,9 +192,8 @@
     blocks_ref,
     counts_ref,
     q_ref,
-    kv_ref,
-    kv_prev_ref,
-    kv_next_ref,
+    ext,
+    grad,
     co_ref,
     ct_ref,
     ow_ref,
@@ -75,11 +204,8 @@
     mix_ref,
     mix_other_ref,
     gow_ref,
-    ext,
     acc,
-    grad,
     attn,
-    sems,
 ):
     tp = lax.axis_index("tp")
     slab = lax.axis_index("slab")
@@ -89,30 +215,11 @@
     planes = tokens // PLANE_TOK
     per_plane = PLANE_TOK // BLK
     total = planes * slabs
-    copies = [
-        pltpu.make_async_copy(kv_prev_ref, ext.at[0:PLANE_TOK], sems.at[0]),
-        pltpu.make_async_copy(kv_ref, ext.at[PLANE_TOK : PLANE_TOK + tokens], sems.at[1]),
-        pltpu.make_async_copy(
-            kv_next_ref, ext.at[PLANE_TOK + tokens : 2 * PLANE_TOK + tokens], sems.at[2]
-        ),
-    ]
-    for copy in copies:
-        copy.start()
     mine, other = part(tp, width), part(1 - tp, width)
-
-    @pl.loop(0, tokens // CHUNK)
-    def _(step):
-        rows = part(step, CHUNK)
-        grad[rows, :] = (
-            mm_nt(co_ref[rows, :], ow_ref[:, mine]) + mm_nt(ct_ref[rows, :], ow_ref[:, other])
-        ).astype(BF16)
 
     @pl.loop(0, acc.shape[0] // BLK)
     def _(step):
         acc[part(step, BLK), :] = jnp.zeros((BLK, 2 * cols), F32)
-
-    for copy in copies:
-        copy.wait()
 
     lane = lax.broadcasted_iota(jnp.int32, (1, cols), 1) // HD
     masks = [(lane == h).astype(F32).astype(BF16) for h in range(heads)]
@@ -174,17 +281,6 @@
             gow_ref[part(index * halves + half, cols), :] = product[
                 :, half * 128 : (half + 1) * 128
             ]
-
-
-def copy_to(src, dst, send, recv, where):
-    return pltpu.make_async_remote_copy(
-        src_ref=src,
-        dst_ref=dst,
-        send_sem=send,
-        recv_sem=recv,
-        device_id=where,
-        device_id_type=MESH,
-    )
 
 
 def backward_kernel(
@@ -495,36 +591,30 @@
     plane = PLANE_TOK
     sds = jax.ShapeDtypeStruct
     params = pltpu.CompilerParams(vmem_limit_bytes=LIMIT)
-    up = [(i, (i + 1) % slabs) for i in range(slabs)]
-    down = [(i, (i - 1) % slabs) for i in range(slabs)]
-
-    def to_next(x):
-        return lax.ppermute(x, "slab", up)
-
-    def to_prev(x):
-        return lax.ppermute(x, "slab", down)
-
-    def swap(x):
-        return lax.ppermute(x, "tp", [(0, 1), (1, 0)])
-
-    tok_prev = to_next(tokens[count - plane :])
-    tok_next = to_prev(tokens[:plane])
-    before = jnp.concatenate([tok_prev, tokens[: count - plane]])
-    after = jnp.concatenate([tokens[plane:], tok_next])
-    before_f, own_f, after_f = before.astype(F32), tokens.astype(F32), after.astype(F32)
-    stem = (stem_taps[0] * before_f + stem_taps[1] * own_f + stem_taps[2] * after_f).astype(BF16)
-    stem_other = swap(stem)
-    cot_other = swap(cotangent)
-
-    q, kv = pl.pallas_call(
-        project_kernel,
-        out_shape=[sds((count, cols), BF16), sds((count, 2 * cols), BF16)],
-        in_specs=[VMEM] * 5,
-        out_specs=[VMEM] * 2,
-        compiler_params=params,
-    )(stem, stem_other, query_weight, key_weight, value_weight)
-    kv_prev = to_next(kv[count - plane :])
-    kv_next = to_prev(kv[:plane])
+    stages = slabs.bit_length() - 1
+    chunks = count // CHUNK
+    edge_chunks = plane // CHUNK
+    dma = pltpu.SemaphoreType.DMA
+    pairs = [(2, edge_chunks)] * 2 + [(chunks,)] * 4 + [(2, edge_chunks)] * 2
+    stem, stem_other, cot_other, tok_prev, tok_next, q, ext, grad = pl.pallas_call(
+        functools.partial(forward_kernel, slabs),
+        out_shape=[
+            sds((count, width), BF16),
+            sds((count, width), BF16),
+            sds((count, width), BF16),
+            sds((plane, width), BF16),
+            sds((plane, width), BF16),
+            sds((count, cols), BF16),
+            sds((count + 2 * plane, 2 * cols), BF16),
+            sds((count, cols), BF16),
+        ],
+        in_specs=[VMEM] * 7,
+        out_specs=[VMEM] * 8,
+        scratch_shapes=[dma(shape) for shape in pairs],
+        compiler_params=pltpu.CompilerParams(
+            collective_id=0, has_side_effects=True, vmem_limit_bytes=LIMIT
+        ),
+    )(tokens, stem_taps, query_weight, key_weight, value_weight, out_weight, cotangent)
 
     gq, gkv, gprev, gnext, mix, mix_other, gow = pl.pallas_call(
         functools.partial(attention_kernel, slabs),
@@ -537,22 +627,15 @@
             sds((count, width), BF16),
             sds((cols * depth // 128, 128), F32),
         ],
-        in_specs=[SMEM, SMEM, VMEM, ANY, ANY, ANY, VMEM, VMEM, VMEM],
+        in_specs=[SMEM, SMEM] + [VMEM] * 6,
         out_specs=[VMEM] * 7,
         scratch_shapes=[
-            pltpu.VMEM((count + 2 * plane, 2 * cols), BF16),
             pltpu.VMEM((count + 2 * plane, 2 * cols), F32),
             pltpu.VMEM((count, cols), BF16),
-            pltpu.VMEM((count, cols), BF16),
-            pltpu.SemaphoreType.DMA((3,)),
         ],
         compiler_params=params,
-    )(key_blocks, counts, q, kv, kv_prev, kv_next, cotangent, cot_other, out_weight)
-    stages = slabs.bit_length() - 1
-    chunks = count // CHUNK
-    edge_chunks = plane // CHUNK
+    )(key_blocks, counts, q, ext, grad, cotangent, cot_other, out_weight)
     rows = 4 * depth * cols // 128
-    dma = pltpu.SemaphoreType.DMA
     layer_out, grad_tokens, final, taps = pl.pallas_call(
         functools.partial(backward_kernel, slabs),
         out_shape=[

time: 130 us -> 116 us (0.89)
  Pallas kernels: 80.4 us -> 111 us
  waiting for transfers between devices: 25.7 us -> 0 us
  starting transfers between devices: 12.4 us -> 0 us
  local copies, waits for them, and re-layouts: 9.11 us -> 4.19 us
  other arithmetic: 1.52 us -> 0 us
    pallas_call x1, Pallas kernels: 3.92 us -> 33.3 us  [body(): pl.pallas_call(functools.partial(forward_kernel, slabs), out_shape=[sds((...]
    ppermute x6 -> x0, waiting for transfers between devices: 25.7 us -> none  [the longest x2 11.7 us: swap(): return lax.ppermute(x, 'tp', [(0, 1), (1, 0)])]
    ppermute x6 -> x0, starting transfers between devices: 12.4 us -> none  [the longest x2 9.67 us: to_prev(): return lax.ppermute(x, 'slab', down)]
    slice x3 -> x0, local copies, waits for them, and re-layouts: 3.99 us -> none  [the longest x1 2.06 us: body(): kv_next = to_prev(kv[:plane])]
    pallas_call x1, Pallas kernels: 54.5 us -> 56.2 us  [body(): pl.pallas_call(functools.partial(backward_kernel, slabs), out_shape=[sds(...]
    convert_element_type x1 -> x0, other arithmetic: 1.52 us -> none  [body(): (stem_taps[0] * before_f + stem_taps[1] * own_f + stem_taps[2] * after_f)...]
    unnamed x23 -> x5, local copies, waits for them, and re-layouts: 5.13 us -> 4.19 us
  transfers between devices with their start and end apart: 6 -> 0, of which waited for: 4 -> 0; matrix products, arithmetic and copies ran while one was open for 3% -> 0% of each run, Pallas kernels for 3% -> 0%
where the time goes in v3:
time: 116 us
  Pallas kernels  111 us (96%)
  local copies, waits for them, and re-layouts  4.19 us (4%)
    pallas_call x1, Pallas kernels, body(): pl.pallas_call(functools.partial(backward_kernel, slabs), out_shape=[sds(...  56.2 us
    pallas_call x1, Pallas kernels, body(): pl.pallas_call(functools.partial(forward_kernel, slabs), out_shape=[sds((...  33.3 us
    pallas_call x1, Pallas kernels, body(): pl.pallas_call(functools.partial(attention_kernel, slabs), out_shape=[sds...  18.9 us
    unnamed x5, local copies, waits for them, and re-layouts  4.19 us
    pallas_call x1, Pallas kernels, body(): pl.pallas_call(unpack_kernel, out_shape=[sds((depth, cols), F32)] * 3 + [...  2.7 us

profile of v3, /device:TPU:0, one launch (start us, length us, event | category | flops | bytes accessed | tf_op | source)
XLA Modules:
  0.0 115.9 jit_solution(281803504412844961)
XLA Ops:
  0.6 1.3 %copy.16.blocks_ref = s32[8,4]{1,0:T(8,128)} copy(s32[8,4]{0,1:T(4,128)} %param.15) | data formatting | bytes 256 | tf_op args[6]
  2.0 33.3 %shard_map.144 = (bf16[1024,256]{1,0:T(8,128)(2,1)}, bf16[1024,256]{1,0:T(8,128)(2,1)}, bf16[1024,256]{1,0:T(8,128)(2,1)}, bf16[512,256]{1,0:T(8,128)(2,1)}, bf1...) custom-call(bf16[1024,256]{1,0:T(8,128)(2,1)} %tok_ref.3, ...), custom_call_target="tpu_custom_call" | custom-call | tf_op jit(solution)/shard_map/pallas_call | solution.py:599
  35.3 18.9 %shard_map.145 = (bf16[1024,256]{1,0:T(8,128)(2,1)}, f32[1024,512]{1,0:T(8,128)}, bf16[512,512]{1,0:T(8,128)(2,1)}, bf16[512,512]{1,0:T(8,128)(2,1)}, f32[1024,2...) custom-call(s32[8,4]{1,0:T(8,128)} %copy.16.blocks_ref, s32[8]{0:T(128)} %counts_ref.1, ...), custom_call_target="tpu_custom_call" | custom-call | tf_op jit(solution)/shard_map/pallas_call | solution.py:619
  54.1 56.2 %shard_map.146 = (bf16[1024,256]{1,0:T(8,128)(2,1)}, f32[1024,256]{1,0:T(8,128)}, bf16[4096,128]{1,0:T(8,128)(2,1)}, f32[8,256]{1,0:T(8,128)}) custom-call(bf16[1024,256]{1,0:T(8,128)(2,1)} %get-tuple-element.35.gq_ref, f32[1024,512]{1,0:T(8,128)} %get-tuple-element.36.gkv_ref, bf16[512,512]{1,0:T(8,128)(2,1)} %get-tuple-element.37.gprev_ref, ...), custom_call_target="tpu_custom_call" | custom-call | tf_op jit(solution)/shard_map/pallas_call | solution.py:639
  110.4 0.0 copy-start
  110.4 2.7 %shard_map.147 = (f32[512,256]{1,0:T(8,128)}, f32[512,256]{1,0:T(8,128)}, f32[512,256]{1,0:T(8,128)}, f32[256,512]{1,0:T(8,128)}, f32[3,256]{1,0:T(4,128)}) custom-call(bf16[4096,128]{1,0:T(8,128)(2,1)} %get-tuple-element.48.final_ref, f32[8,256]{1,0:T(8,128)} %get-tuple-element.49.taps_in_ref), custom_call_target="tpu_custom_call" | custom-call | tf_op jit(solution)/shard_map/pallas_call | solution.py:701
  113.1 1.9 %copy.19 = bf16[1024,256]{1,0:T(8,128)(2,1)} copy(bf16[1024,256]{1,0:T(8,128)(2,1)} %get-tuple-element.62) | data formatting | bytes 1048576
  115.0 0.0 copy-done
  115.0 1.0 copy.20
Async XLA Ops:
  110.4 4.6 %copy-start = (f32[1024,256]{1,0:T(8,128)S(1)}, f32[1024,256]{1,0:T(8,128)}, u32[]{:S(2)}) copy-start(f32[1024,256]{1,0:T(8,128)} %get-tuple-element.63) | copy-start | bytes 3145732

commit v4 on v3

--- a/solution.py
+++ b/solution.py
@@ -17,7 +17,7 @@
 MESH = pl.DeviceIdType.MESH
 VMEM = pl.BlockSpec(memory_space=pltpu.VMEM)
 SMEM = pl.BlockSpec(memory_space=pltpu.SMEM)
-LIMIT = 60 * 1024 * 1024
+MIB = 1024 * 1024
 CHUNK = 256
 
 
@@ -223,23 +223,22 @@
 
     lane = lax.broadcasted_iota(jnp.int32, (1, cols), 1) // HD
     masks = [(lane == h).astype(F32).astype(BF16) for h in range(heads)]
-    slot = lax.broadcasted_iota(jnp.int32, (1, MAXK * BLK), 1)
 
     def stack(block):
         return jnp.concatenate([block * mask for mask in masks], axis=0)
 
     def pick(value):
-        out = value[0:BLK]
-        for h in range(1, heads):
-            out = jnp.where(lane == h, value[h * BLK : (h + 1) * BLK], out)
-        return out
+        heads_t = [
+            value[h * HD : (h + 1) * HD, h * BLK : (h + 1) * BLK] for h in range(heads)
+        ]
+        return jnp.concatenate(heads_t, axis=0).T
 
     @pl.loop(0, tokens // BLK)
     def _(i):
         rows = part(i, BLK)
         where = []
         for j in range(MAXK):
-            block = blocks_ref[i, j]
+            block = blocks_ref[j, i]
             plane = lax.rem(
                 lax.div(block, per_plane) - slab * planes + 1 + total, total
             )
@@ -248,18 +247,25 @@
         values = jnp.concatenate([ext[at, cols : 2 * cols] for at in where], axis=0)
         queries = stack(q_ref[rows, :] * jnp.asarray(HD**-0.5, BF16))
         grads = stack(grad[rows, :])
-        scores = mm_nt(queries, keys)
-        scores = jnp.where(slot < counts_ref[i] * BLK, scores, NEG)
-        exps = jnp.exp(scores - jnp.max(scores, axis=-1, keepdims=True))
-        probs = exps * (1.0 / jnp.sum(exps, axis=-1, keepdims=True))
+        scores = mm_nt(keys, queries)
+        live = counts_ref[i]
+        scores = jnp.concatenate(
+            [
+                jnp.where(j < live, scores[j * BLK : (j + 1) * BLK], NEG)
+                for j in range(MAXK)
+            ],
+            axis=0,
+        )
+        exps = jnp.exp(scores - jnp.max(scores, axis=0, keepdims=True))
+        probs = exps * (1.0 / jnp.sum(exps, axis=0, keepdims=True))
         low = probs.astype(BF16)
-        attn[rows, :] = pick(mm(low, values)).astype(BF16)
-        gprobs = mm_nt(grads, values)
-        inner = jnp.sum(probs * gprobs, axis=-1, keepdims=True)
+        attn[rows, :] = pick(mm_tn(values, low)).astype(BF16)
+        gprobs = mm_nt(values, grads)
+        inner = jnp.sum(probs * gprobs, axis=0, keepdims=True)
         gscores = (probs * (gprobs - inner)).astype(BF16)
-        gq_ref[rows, :] = (pick(mm(gscores, keys)) * (HD**-0.5)).astype(BF16)
-        gkeys = mm_tn(gscores, queries)
-        gvalues = mm_tn(low, grads)
+        gq_ref[rows, :] = (pick(mm_tn(keys, gscores)) * (HD**-0.5)).astype(BF16)
+        gkeys = mm(gscores, queries)
+        gvalues = mm(low, grads)
         for j in range(MAXK):
             acc[where[j], 0:cols] += gkeys[j * BLK : (j + 1) * BLK]
             acc[where[j], cols : 2 * cols] += gvalues[j * BLK : (j + 1) * BLK]
@@ -339,7 +345,7 @@
     tp = lax.axis_index("tp")
     bits = tuple(range(slabs.bit_length() - 1))
     stages = len(bits)
-    orders = (bits, bits[:1] + bits[2:] + bits[1:2])
+    orders = (bits[:1] + bits[2:] + bits[1:2], bits)
     tokens, cols = gq_ref.shape
     width = so_ref.shape[1]
     depth = wq_ref.shape[0]
@@ -442,6 +448,7 @@
         gq = gq_ref[rows, :]
         own[rows, :] = mm_nt(gq, wq_ref[mine, :])
         other[rows, :] = mm_nt(gq, wq_ref[theirs, :])
+    advance(0)
     advance(0)
     down.wait_recv()
     up.wait_recv()
@@ -590,7 +597,7 @@
     depth, cols = query_weight.shape
     plane = PLANE_TOK
     sds = jax.ShapeDtypeStruct
-    params = pltpu.CompilerParams(vmem_limit_bytes=LIMIT)
+    params = pltpu.CompilerParams(vmem_limit_bytes=20 * MIB)
     stages = slabs.bit_length() - 1
     chunks = count // CHUNK
     edge_chunks = plane // CHUNK
@@ -612,7 +619,7 @@
         out_specs=[VMEM] * 8,
         scratch_shapes=[dma(shape) for shape in pairs],
         compiler_params=pltpu.CompilerParams(
-            collective_id=0, has_side_effects=True, vmem_limit_bytes=LIMIT
+            collective_id=0, has_side_effects=True, vmem_limit_bytes=16 * MIB
         ),
     )(tokens, stem_taps, query_weight, key_weight, value_weight, out_weight, cotangent)
 
@@ -634,7 +641,7 @@
             pltpu.VMEM((count, cols), BF16),
         ],
         compiler_params=params,
-    )(key_blocks, counts, q, ext, grad, cotangent, cot_other, out_weight)
+    )(key_blocks.T, counts, q, ext, grad, cotangent, cot_other, out_weight)
     rows = 4 * depth * cols // 128
     layer_out, grad_tokens, final, taps = pl.pallas_call(
         functools.partial(backward_kernel, slabs),
@@ -677,7 +684,7 @@
             dma((stages,)),
         ],
         compiler_params=pltpu.CompilerParams(
-            collective_id=1, has_side_effects=True, vmem_limit_bytes=LIMIT
+            collective_id=1, has_side_effects=True, vmem_limit_bytes=30 * MIB
         ),
     )(
         gq,

time: 116 us -> 105 us (0.905)
  Pallas kernels: 111 us -> 95.4 us
  local copies, waits for them, and re-layouts: 4.19 us -> 8.38 us
    pallas_call x1, Pallas kernels: 56.2 us -> 49 us  [body(): pl.pallas_call(functools.partial(backward_kernel, slabs), out_shape=[sds(...]
    unnamed x5 -> x34, local copies, waits for them, and re-layouts: 4.19 us -> 8.38 us
    pallas_call x1, Pallas kernels: 33.3 us -> 29.5 us  [body(): pl.pallas_call(functools.partial(forward_kernel, slabs), out_shape=[sds((...]
    pallas_call x1, Pallas kernels: 18.9 us -> 15.4 us  [body(): pl.pallas_call(functools.partial(attention_kernel, slabs), out_shape=[sds...]
    pallas_call x1, Pallas kernels: 2.7 us -> 1.44 us  [body(): pl.pallas_call(unpack_kernel, out_shape=[sds((depth, cols), F32)] * 3 + [...]
where the time goes in v4:
time: 105 us
  Pallas kernels  95.4 us (91%)
  local copies, waits for them, and re-layouts  8.38 us (8%)
    pallas_call x1, Pallas kernels, body(): pl.pallas_call(functools.partial(backward_kernel, slabs), out_shape=[sds(...  49 us
    pallas_call x1, Pallas kernels, body(): pl.pallas_call(functools.partial(forward_kernel, slabs), out_shape=[sds((...  29.5 us
    pallas_call x1, Pallas kernels, body(): pl.pallas_call(functools.partial(attention_kernel, slabs), out_shape=[sds...  15.4 us
    unnamed x34, local copies, waits for them, and re-layouts  8.38 us

profile of v4, /device:TPU:0, one launch (start us, length us, event | category | flops | bytes accessed | tf_op | source)
XLA Modules:
  0.0 104.5 jit_solution(11836828194070764034)
XLA Ops:
  0.6 0.0 copy-start.15
  0.6 0.0 copy-start
  0.7 1.0 copy-done
  1.7 0.0 copy-start.2
  1.7 1.0 copy-done.2
  2.7 0.0 copy-start.4
  2.7 0.9 copy-done.4
  3.7 0.0 copy-start.6
  3.7 0.9 copy-done.6
  4.6 0.9 copy-done.8
  5.6 0.9 copy-done.10
  6.5 0.7 copy-done.12
  7.2 29.5 %shard_map.144 = (bf16[1024,256]{1,0:T(8,128)(2,1)S(1)}, bf16[1024,256]{1,0:T(8,128)(2,1)S(1)}, bf16[1024,256]{1,0:T(8,128)(2,1)S(1)}, bf16[512,256]{1,0:T(8,128...) custom-call(bf16[1024,256]{1,0:T(8,128)(2,1)S(1)} %copy-done.2, ...), custom_call_target="tpu_custom_call" | custom-call | tf_op jit(solution)/shard_map/pallas_call | solution.py:606
  36.7 0.0 copy-done.15
  36.7 0.0 copy-done.1
  36.8 0.0 copy-done.5
  36.8 0.0 copy-done.14
  36.8 0.0 copy-start.3
  36.8 0.0 copy-start.7
  36.8 0.0 copy-start.9
  36.8 0.0 copy-start.11
  36.8 0.0 copy-start.13
  36.8 15.4 %shard_map.145 = (bf16[1024,256]{1,0:T(8,128)(2,1)S(1)}, f32[1024,512]{1,0:T(8,128)S(1)}, bf16[512,512]{1,0:T(8,128)(2,1)S(1)}, bf16[512,512]{1,0:T(8,128)(2,1)S...) custom-call(s32[4,8]{1,0:T(4,128)S(1)} %bitcast.1, s32[8]{0:T(128)S(1)} %copy-done.15, ...), custom_call_target="tpu_custom_call" | custom-call | tf_op jit(solution)/shard_map/pallas_call | solution.py:626
  52.3 0.0 copy-done.3
  52.3 0.0 copy-done.7
  52.3 0.0 copy-done.9
  52.3 0.0 copy-done.11
  52.3 0.0 copy-done.13
  52.3 49.0 %shard_map.146 = (bf16[1024,256]{1,0:T(8,128)(2,1)S(1)}, f32[1024,256]{1,0:T(8,128)S(1)}, bf16[4096,128]{1,0:T(8,128)(2,1)S(1)}, f32[8,256]{1,0:T(8,128)S(1)}) custom-call(bf16[1024,256]{1,0:T(8,128)(2,1)S(1)} %get-tuple-element.35.gq_ref, f32[1024,512]{1,0:T(8,128)S(1)} %get-tuple-element.36.gkv_ref, bf16[512,512]{1,0:T(8,128)(2,1)S(1)} %get-tuple-element.37.gprev_ref, ...), custom_call_target="tpu_custom_call" | custom-call | tf_op jit(solution)/shard_map/pallas_call | solution.py:646
  101.3 1.4 %shard_map.147 = (f32[512,256]{1,0:T(8,128)}, f32[512,256]{1,0:T(8,128)}, f32[512,256]{1,0:T(8,128)}, f32[256,512]{1,0:T(8,128)}, f32[3,256]{1,0:T(4,128)}) custom-call(bf16[4096,128]{1,0:T(8,128)(2,1)S(1)} %get-tuple-element.48.final_ref, f32[8,256]{1,0:T(8,128)S(1)} %get-tuple-element.49.taps_in_ref), custom_call_target="tpu_custom_call" | custom-call | tf_op jit(solution)/shard_map/pallas_call | solution.py:708
  102.8 0.8 copy.18
  103.5 1.0 copy.19
  (6 shorter events, 0.0 us)
Async XLA Ops:
  0.6 36.1 %copy-start.15 = (s32[8]{0:T(128)S(1)}, s32[8]{0:T(128)}, u32[]{:S(2)}) copy-start(s32[8]{0:T(128)} %counts_ref.1) | copy-start | bytes 100
  0.6 1.0 %copy-start = (bf16[1024,256]{1,0:T(8,128)(2,1)S(1)}, bf16[1024,256]{1,0:T(8,128)(2,1)}, u32[]{:S(2)}) copy-start(bf16[1024,256]{1,0:T(8,128)(2,1)} %cot_ref.3) | copy-start | bytes 1572868
  1.7 1.0 copy-start.2
  2.7 0.9 copy-start.4
  3.7 0.9 copy-start.6
  4.6 0.9 copy-start.8
  5.6 0.9 copy-start.10
  6.5 0.7 copy-start.12
  7.2 29.5 %copy-start.1 = (bf16[1024,256]{1,0:T(8,128)(2,1)S(1)}, bf16[1024,256]{1,0:T(8,128)(2,1)}, u32[]{:S(2)}) copy-start(bf16[1024,256]{1,0:T(8,128)(2,1)} %cot_ref.3) | copy-start | bytes 1572868
  7.2 29.5 %copy-start.5 = (bf16[256,512]{1,0:T(8,128)(2,1)S(1)}, bf16[256,512]{1,0:T(8,128)(2,1)}, u32[]{:S(2)}) copy-start(bf16[256,512]{1,0:T(8,128)(2,1)} %ow_ref.3) | copy-start | bytes 786436
  7.2 29.5 %copy-start.14 = (s32[8,4]{0,1:T(4,128)S(1)}, s32[8,4]{0,1:T(4,128)}, u32[]{:S(2)}) copy-start(s32[8,4]{0,1:T(4,128)} %param.15) | copy-start | bytes 388
  36.8 15.5 %copy-start.3 = (bf16[1024,256]{1,0:T(8,128)(2,1)S(1)}, bf16[1024,256]{1,0:T(8,128)(2,1)}, u32[]{:S(2)}) copy-start(bf16[1024,256]{1,0:T(8,128)(2,1)} %tok_ref.3) | copy-start | bytes 1572868
  36.8 15.5 %copy-start.7 = (bf16[512,256]{1,0:T(8,128)(2,1)S(1)}, bf16[512,256]{1,0:T(8,128)(2,1)}, u32[]{:S(2)}) copy-start(bf16[512,256]{1,0:T(8,128)(2,1)} %wq_ref.3) | copy-start | bytes 786436
  36.8 15.5 %copy-start.9 = (bf16[512,256]{1,0:T(8,128)(2,1)S(1)}, bf16[512,256]{1,0:T(8,128)(2,1)}, u32[]{:S(2)}) copy-start(bf16[512,256]{1,0:T(8,128)(2,1)} %wk_ref.3) | copy-start | bytes 786436
  36.8 15.5 %copy-start.11 = (bf16[512,256]{1,0:T(8,128)(2,1)S(1)}, bf16[512,256]{1,0:T(8,128)(2,1)}, u32[]{:S(2)}) copy-start(bf16[512,256]{1,0:T(8,128)(2,1)} %wv_ref.3) | copy-start | bytes 786436
  36.8 15.5 %copy-start.13 = (f32[3,256]{1,0:T(4,128)S(1)}, f32[3,256]{1,0:T(4,128)}, u32[]{:S(2)}) copy-start(f32[3,256]{1,0:T(4,128)} %taps_ref.3) | copy-start | bytes 9220

commit v5 on v4

--- a/solution.py
+++ b/solution.py
@@ -50,13 +50,9 @@
 
 def forward_kernel(
     slabs,
-    tok_ref,
+    all_ref,
     taps_ref,
-    wq_ref,
-    wk_ref,
-    wv_ref,
     ow_ref,
-    cot_ref,
     so_ref,
     st_ref,
     ct_ref,
@@ -76,8 +72,13 @@
 ):
     me = lax.axis_index("slab")
     tp = lax.axis_index("tp")
-    tokens, width = tok_ref.shape
-    cols = wq_ref.shape[1]
+    tokens, width = so_ref.shape
+    cols, depth = ow_ref.shape
+    tok_ref = all_ref.at[0:tokens]
+    cot_ref = all_ref.at[tokens : 2 * tokens]
+    wq_ref, wk_ref, wv_ref = (
+        all_ref.at[2 * tokens + n * depth : 2 * tokens + (n + 1) * depth] for n in range(3)
+    )
     chunks = tokens // CHUNK
     edge_chunks = PLANE_TOK // CHUNK
     last = tokens - PLANE_TOK
@@ -615,13 +616,17 @@
             sds((count + 2 * plane, 2 * cols), BF16),
             sds((count, cols), BF16),
         ],
-        in_specs=[VMEM] * 7,
+        in_specs=[VMEM] * 3,
         out_specs=[VMEM] * 8,
         scratch_shapes=[dma(shape) for shape in pairs],
         compiler_params=pltpu.CompilerParams(
             collective_id=0, has_side_effects=True, vmem_limit_bytes=16 * MIB
         ),
-    )(tokens, stem_taps, query_weight, key_weight, value_weight, out_weight, cotangent)
+    )(
+        jnp.concatenate([tokens, cotangent, query_weight, key_weight, value_weight]),
+        stem_taps,
+        out_weight,
+    )
 
     gq, gkv, gprev, gnext, mix, mix_other, gow = pl.pallas_call(
         functools.partial(attention_kernel, slabs),

time: 105 us -> 101 us (0.962)
  local copies, waits for them, and re-layouts: 8.38 us -> 4.1 us
    unnamed x34 -> x24, local copies, waits for them, and re-layouts: 8.38 us -> 4.08 us
where the time goes in v5:
time: 101 us
  Pallas kernels  95.6 us (95%)
  local copies, waits for them, and re-layouts  4.1 us (4%)
    pallas_call x1, Pallas kernels, body(): pl.pallas_call(functools.partial(backward_kernel, slabs), out_shape=[sds(...  49 us
    pallas_call x1, Pallas kernels, body(): pl.pallas_call(functools.partial(forward_kernel, slabs), out_shape=[sds((...  29.5 us
    pallas_call x1, Pallas kernels, body(): pl.pallas_call(functools.partial(attention_kernel, slabs), out_shape=[sds...  15.6 us
    unnamed x24, local copies, waits for them, and re-layouts  4.08 us

profile of v5, /device:TPU:0, one launch (start us, length us, event | category | flops | bytes accessed | tf_op | source)
XLA Modules:
  0.0 100.5 jit_solution(13129297867265114404)
XLA Ops:
  0.6 0.0 copy-start.4
  0.6 0.0 copy-start.3
  0.7 0.0 copy-start.2
  0.7 0.0 copy-start.5
  0.7 0.0 copy-start.6
  0.7 1.2 %constant_dynamic-update-slice_fusion.4 = bf16[3584,256]{1,0:T(8,128)(2,1)S(1)} fusion(bf16[1024,256]{1,0:T(8,128)(2,1)} %tok_ref.1), kind=kLoop, calls=%fused_computation.4 | loop fusion | bytes 1048576
  1.8 1.1 %constant_dynamic-update-slice_fusion.3 = bf16[3584,256]{1,0:T(8,128)(2,1)S(1)} fusion(bf16[3584,256]{1,0:T(8,128)(2,1)S(1)} %constant_dynamic-update-slice_fusion.4, bf16[1024,256]{1,0:T(8,128)(2,1)} %cot_ref.1), kind=kLoop, calls=%fused_computation.3 | loop fusion | bytes 1048576
  2.9 0.0 copy-done.2
  2.9 0.0 copy-start
  2.9 0.0 copy-start.7
  3.0 0.0 copy-start.8
  3.0 0.0 copy-done.3
  3.0 0.0 copy-done.4
  3.1 0.0 copy-done.5
  3.1 0.0 copy-done.6
  3.1 29.5 %shard_map.144 = (bf16[1024,256]{1,0:T(8,128)(2,1)S(1)}, bf16[1024,256]{1,0:T(8,128)(2,1)S(1)}, bf16[1024,256]{1,0:T(8,128)(2,1)S(1)}, bf16[512,256]{1,0:T(8,128...) custom-call(bf16[3584,256]{1,0:T(8,128)(2,1)S(1)} %constant_dynamic-, ...), custom_call_target="tpu_custom_call" | custom-call | tf_op jit(solution)/shard_map/pallas_call | solution.py:607
  32.6 0.0 copy-done
  32.7 0.0 copy-done.7
  32.7 0.0 copy-done.8
  32.7 0.0 copy-start.1
  32.7 15.6 %shard_map.145 = (bf16[1024,256]{1,0:T(8,128)(2,1)S(1)}, f32[1024,512]{1,0:T(8,128)S(1)}, bf16[512,512]{1,0:T(8,128)(2,1)S(1)}, bf16[512,512]{1,0:T(8,128)(2,1)S...) custom-call(s32[4,8]{1,0:T(4,128)S(1)} %bitcast.1, s32[8]{0:T(128)S(1)} %copy-done.8, ...), custom_call_target="tpu_custom_call" | custom-call | tf_op jit(solution)/shard_map/pallas_call | solution.py:631
  48.3 0.0 copy-done.1
  48.3 49.0 %shard_map.146 = (bf16[1024,256]{1,0:T(8,128)(2,1)S(1)}, f32[1024,256]{1,0:T(8,128)S(1)}, bf16[4096,128]{1,0:T(8,128)(2,1)S(1)}, f32[8,256]{1,0:T(8,128)S(1)}) custom-call(bf16[1024,256]{1,0:T(8,128)(2,1)S(1)} %get-tuple-element.35.gq_ref, f32[1024,512]{1,0:T(8,128)S(1)} %get-tuple-element.36.gkv_ref, bf16[512,512]{1,0:T(8,128)(2,1)S(1)} %get-tuple-element.37.gprev_ref, ...), custom_call_target="tpu_custom_call" | custom-call | tf_op jit(solution)/shard_map/pallas_call | solution.py:651
  97.3 1.4 %shard_map.147 = (f32[512,256]{1,0:T(8,128)}, f32[512,256]{1,0:T(8,128)}, f32[512,256]{1,0:T(8,128)}, f32[256,512]{1,0:T(8,128)}, f32[3,256]{1,0:T(4,128)}) custom-call(bf16[4096,128]{1,0:T(8,128)(2,1)S(1)} %get-tuple-element.48.final_ref, f32[8,256]{1,0:T(8,128)S(1)} %get-tuple-element.49.taps_in_ref), custom_call_target="tpu_custom_call" | custom-call | tf_op jit(solution)/shard_map/pallas_call | solution.py:713
  98.8 0.8 copy.22
  99.5 1.0 copy.23
  (3 shorter events, 0.1 us)
Async XLA Ops:
  0.6 2.4 %copy-start.4 = (bf16[512,256]{1,0:T(8,128)(2,1)S(1)}, bf16[512,256]{1,0:T(8,128)(2,1)}, u32[]{:S(2)}) copy-start(bf16[512,256]{1,0:T(8,128)(2,1)} %wv_ref.1) | copy-start | bytes 786436
  0.6 2.4 %copy-start.3 = (bf16[512,256]{1,0:T(8,128)(2,1)S(1)}, bf16[512,256]{1,0:T(8,128)(2,1)}, u32[]{:S(2)}) copy-start(bf16[512,256]{1,0:T(8,128)(2,1)} %wk_ref.1) | copy-start | bytes 786436
  0.7 2.3 %copy-start.2 = (bf16[512,256]{1,0:T(8,128)(2,1)S(1)}, bf16[512,256]{1,0:T(8,128)(2,1)}, u32[]{:S(2)}) copy-start(bf16[512,256]{1,0:T(8,128)(2,1)} %wq_ref.1) | copy-start | bytes 786436
  0.7 2.4 %copy-start.5 = (bf16[256,512]{1,0:T(8,128)(2,1)S(1)}, bf16[256,512]{1,0:T(8,128)(2,1)}, u32[]{:S(2)}) copy-start(bf16[256,512]{1,0:T(8,128)(2,1)} %ow_ref.3) | copy-start | bytes 786436
  0.7 2.4 %copy-start.6 = (f32[3,256]{1,0:T(4,128)S(1)}, f32[3,256]{1,0:T(4,128)}, u32[]{:S(2)}) copy-start(f32[3,256]{1,0:T(4,128)} %taps_ref.3) | copy-start | bytes 9220
  2.9 29.7 %copy-start = (bf16[1024,256]{1,0:T(8,128)(2,1)S(1)}, bf16[1024,256]{1,0:T(8,128)(2,1)}, u32[]{:S(2)}) copy-start(bf16[1024,256]{1,0:T(8,128)(2,1)} %cot_ref.1) | copy-start | bytes 1572868
  2.9 29.7 %copy-start.7 = (s32[8,4]{0,1:T(4,128)S(1)}, s32[8,4]{0,1:T(4,128)}, u32[]{:S(2)}) copy-start(s32[8,4]{0,1:T(4,128)} %param.15) | copy-start | bytes 388
  3.0 29.7 %copy-start.8 = (s32[8]{0:T(128)S(1)}, s32[8]{0:T(128)}, u32[]{:S(2)}) copy-start(s32[8]{0:T(128)} %counts_ref.1) | copy-start | bytes 100
  32.7 15.6 %copy-start.1 = (bf16[1024,256]{1,0:T(8,128)(2,1)S(1)}, bf16[1024,256]{1,0:T(8,128)(2,1)}, u32[]{:S(2)}) copy-start(bf16[1024,256]{1,0:T(8,128)(2,1)} %tok_ref.1) | copy-start | bytes 1572868
